TPU v7x, 32 devices: a whole 2x2x4 slice. The times are simulated.
32 devices in a mesh: parts: 2 (over x), row: 16 (over z, y, core).
Axes of the slice: x: 2, y: 2, z: 4, core: 2. Of those that a mesh axis runs over, the one named last changes fastest.
Arguments:
- coords: int32 [4, 3, 512], P('parts'), parts along dimension 0, may hold values from 0 to 7
- labels: int32 [16, 16, 512], P('parts', 'row'), parts along dimension 0, may hold values from 0 to 255
- ranks: int32 [16, 16, 2], P('parts', 'row'), parts along dimension 0, may hold values from 16 to 128, as said below
- u_first: bfloat16 [16, 16, 512, 128], P('parts', 'row'), parts along dimension 0, may hold values from -6 to 6
- v_first: bfloat16 [16, 16, 512, 128], P('parts', 'row'), parts along dimension 0, may hold values from -0.0046875 to 0.0046875
- u_second: bfloat16 [16, 16, 512, 128], P('parts', 'row'), parts along dimension 0, may hold values from -6 to 6
- v_second: bfloat16 [16, 16, 512, 128], P('parts', 'row'), parts along dimension 0, may hold values from -0.01171875 to 0.01171875
Outputs:
- eliminated: float32 [16, 16, 512, 256], P('parts', 'row'), parts along dimension 0
- diagonal_factors: float32 [4, 512, 512], P('parts'), parts along dimension 0
There are 2 independent parts, one for each index of `parts`. A program takes and returns all parts, laid end to end along the dimension named above; each array names one. Nothing has to cross between parts.
Inputs may be any that keep to these rules, and one draw needn't show every extreme that they name: `ranks`: the block of tile 1 in column 0 has rank 128; some block has rank 128 // 8.
All inputs are finite; a program needn't handle non-finite values.
Results may differ from a plain program's by a relative error of at most 0.0003.
Values may be sent and summed in bfloat16 or wider, within the bound.
No kernel may reach another device: no remote copies, remote signals or barrier semaphores. Data moves between devices by JAX's collectives and lax.ppermute only.
A program may use at most 128 MiB of HBM per device.

v0:
```python
import math

import jax
import jax.numpy as jnp
from jax import lax
from jax.sharding import PartitionSpec as P

NRHS = 256


highest = lax.Precision.HIGHEST
four_pi = 4.0 * math.pi


def spread(shard, axis, root):
    mine = lax.axis_index(axis) == root
    return lax.psum(jnp.where(mine, shard, jnp.zeros_like(shard)), axis)


def matmul(left, right):
    return jnp.dot(left, right, precision=highest, preferred_element_type=jnp.float32)


def kernel_tile(points):
    spots = points.astype(jnp.float32)
    distance = jnp.zeros((spots.shape[1], spots.shape[1]), jnp.float32)
    for dimension in range(3):
        offset = spots[dimension][:, None] - spots[dimension][None, :]
        distance = distance + offset * offset
    return 1.0 / (four_pi * jnp.sqrt(distance + 1.0)) + jnp.eye(spots.shape[1], dtype=jnp.float32)


def onehot(label_row):
    return (label_row[..., None] == jnp.arange(NRHS, dtype=jnp.int32)).astype(jnp.float32)


def triangular(lower, target):
    return lax.linalg.triangular_solve(lower, target, left_side=True, lower=True)


def solve_stack(lower, stack):
    number, height, breadth = stack.shape
    flat = jnp.transpose(stack, (1, 0, 2)).reshape(height, number * breadth)
    solved = triangular(lower, flat)
    return jnp.transpose(solved.reshape(height, number, breadth), (1, 0, 2))


def rank_mask(rank_values, breadth):
    columns = jnp.arange(breadth, dtype=jnp.int32)
    return (columns[None, :] < rank_values[:, None]).astype(jnp.float32)


def second_panel(points, label_row, u_one, w_one, first_sol):
    inner_gram = matmul(w_one.T, w_one)
    diagonal_tile = kernel_tile(points) - matmul(matmul(u_one, inner_gram), u_one.T)
    lower = jnp.linalg.cholesky(diagonal_tile)
    target = onehot(label_row) - matmul(u_one, matmul(w_one.T, first_sol))
    return (lower, triangular(lower, target))


def update(
    w_tiles, first_sol, second_lower, second_sol, u_one, w_one, label_rows, rank_rows, u0, u1, v1
):
    breadth = u0.shape[-1]
    u_zero = u0.astype(jnp.float32)
    u_next = u1.astype(jnp.float32)
    v_next = v1.astype(jnp.float32) * rank_mask(rank_rows[:, 1], breadth)[:, None, :]
    first_weights = jnp.einsum("nbr,bc->nrc", w_tiles, first_sol, precision=highest)
    first_update = jnp.einsum("nbr,nrc->nbc", u_zero, first_weights, precision=highest)
    cross = jnp.einsum("br,nbs->nrs", w_one, w_tiles, precision=highest)
    mixed = -jnp.einsum("br,nrs->nbs", u_one, cross, precision=highest)
    factor = solve_stack(second_lower, jnp.concatenate([v_next, mixed], axis=-1))
    second_weights = jnp.einsum("nbk,bc->nkc", factor, second_sol, precision=highest)
    left_pair = jnp.concatenate([u_next, u_zero], axis=-1)
    second_update = jnp.einsum("nbk,nkc->nbc", left_pair, second_weights, precision=highest)
    return onehot(label_rows) - first_update - second_update


def local(coords, labels, ranks, u_first, v_first, u_second, v_second):
    position = lax.axis_index("row")
    label_rows = labels[:, 0]
    rank_rows = ranks[:, 0]
    u_zero = u_first[:, 0]
    v_zero = v_first[:, 0]
    height = u_zero.shape[1]
    breadth = u_zero.shape[2]
    w_tiles = None

    def first_factor():
        lower = jnp.linalg.cholesky(kernel_tile(coords[0]))
        return (lower, triangular(lower, onehot(label_rows[0])))

    def first_empty():
        return (jnp.zeros((height, height), jnp.float32), jnp.zeros((height, NRHS), jnp.float32))

    first_lower, first_sol = lax.cond(position == 0, first_factor, first_empty)
    first_lower, first_sol = (spread(first_lower, "row", 0), spread(first_sol, "row", 0))
    masked = v_zero.astype(jnp.float32) * rank_mask(rank_rows[:, 0], breadth)[:, None, :]
    w_tiles = solve_stack(first_lower, masked)

    def second_factor():
        u_pick = u_zero[0].astype(jnp.float32)
        w_pick = w_tiles[0]
        lower, solved = second_panel(coords[1], label_rows[0], u_pick, w_pick, first_sol)
        return (lower, solved, u_pick, w_pick)

    def second_empty():
        return (
            jnp.zeros((height, height), jnp.float32),
            jnp.zeros((height, NRHS), jnp.float32),
            jnp.zeros((height, breadth), jnp.float32),
            jnp.zeros((height, breadth), jnp.float32),
        )

    second_lower, second_sol, u_one, w_one = lax.cond(position == 1, second_factor, second_empty)
    second_lower, second_sol, u_one, w_one = (
        spread(second_lower, "row", 1),
        spread(second_sol, "row", 1),
        spread(u_one, "row", 1),
        spread(w_one, "row", 1),
    )
    updated = update(
        w_tiles,
        first_sol,
        second_lower,
        second_sol,
        u_one,
        w_one,
        label_rows,
        rank_rows,
        u_zero,
        u_second[:, 0],
        v_second[:, 0],
    )
    leading = jnp.where(position == 0, first_sol, jnp.where(position == 1, second_sol, updated[0]))
    updated = updated.at[0].set(leading)
    return (updated[:, None], jnp.stack([first_lower, second_lower]))


def solution(mesh):
    in_specs = (
        P("parts", None, None),
        P("parts", "row", None),
        P("parts", "row", None),
        P("parts", "row", None, None),
        P("parts", "row", None, None),
        P("parts", "row", None, None),
        P("parts", "row", None, None),
    )
    out_specs = (P("parts", "row", None, None), P("parts", None, None))
    return jax.shard_map(local, mesh=mesh, in_specs=in_specs, out_specs=out_specs, check_vma=False)
```

profile of v0, /device:TPU:0, one launch (start us, length us, event | category | flops | bytes accessed | tf_op | source)
XLA Modules:
  0.0 670.5 jit_solution(9478993667882919614)
XLA Ops:
  7.9 145.0 %conditional.2 = (f32[512,512]{1,0:T(8,128)S(1)}, f32[512,256]{0,1:T(8,128)}) conditional(s32[]{:T(128)} %convert_element_type.64, () %tuple.30, (s32[2,3,512]{2,0,1:T(2,128)}, s32[8,512]{1,0:T(8,128)S(1)}) %tuple.157), branch_computations={%region_0.0_spmd, %region_1.12_spmd} | conditional | flops 916293632 | bytes 19471616 | solution.py:96
  11.5 11.7 %cholesky.286 = f32[128,128]{1,0:T(8,128)S(1)} custom-call(f32[128,128]{1,0:T(8,128)S(1)} %cholesky.426), custom_call_target="Cholesky" | custom-call | tf_op jit(solution)/shard_map/cond/branch_1_fun/jit(cholesky)/cholesky | solution.py:90
  23.3 9.8 %custom-call.35 = f32[1,128,128]{1,2,0:T(8,128)S(1)} custom-call(f32[1,128,128]{2,1,0:T(8,128)S(1)} %get-tuple-element.160), custom_call_target="InvertDiagBlocksLowerTriangular" | custom-call | tf_op jit(solution)/shard_map/cond/branch_1_fun/jit(cholesky)/cholesky | solution.py:90
  33.9 12.0 %cholesky.305 = f32[128,128]{1,0:T(8,128)S(1)} custom-call(f32[128,128]{1,0:T(8,128)S(1)} %cholesky.430), custom_call_target="Cholesky" | custom-call | tf_op jit(solution)/shard_map/cond/branch_1_fun/jit(cholesky)/cholesky | solution.py:90
  47.9 9.8 %custom-call.36 = f32[1,128,128]{1,2,0:T(8,128)S(1)} custom-call(f32[1,128,128]{2,1,0:T(8,128)S(1)} %get-tuple-element.157), custom_call_target="InvertDiagBlocksLowerTriangular" | custom-call | tf_op jit(solution)/shard_map/cond/branch_1_fun/jit(cholesky)/cholesky | solution.py:90
  58.4 11.7 %cholesky.326 = f32[128,128]{1,0:T(8,128)S(1)} custom-call(f32[128,128]{1,0:T(8,128)S(1)} %cholesky.435), custom_call_target="Cholesky" | custom-call | tf_op jit(solution)/shard_map/cond/branch_1_fun/jit(cholesky)/cholesky | solution.py:90
  71.5 9.8 %custom-call.37 = f32[1,128,128]{1,2,0:T(8,128)S(1)} custom-call(f32[1,128,128]{2,1,0:T(8,128)S(1)} %get-tuple-element.154), custom_call_target="InvertDiagBlocksLowerTriangular" | custom-call | tf_op jit(solution)/shard_map/cond/branch_1_fun/jit(cholesky)/cholesky | solution.py:90
  81.9 11.7 %cholesky.343 = f32[128,128]{1,0:T(8,128)S(1)} custom-call(f32[128,128]{1,0:T(8,128)S(1)} %convolution_subtract_fusion.5), custom_call_target="Cholesky" | custom-call | tf_op jit(solution)/shard_map/cond/branch_1_fun/jit(cholesky)/cholesky | solution.py:90
  95.3 10.6 %while.7 = (s32[]{:T(128)}, f32[512,512]{1,0:T(8,128)S(1)}, s32[4,2]{0,1:T(2,128)S(1)}, f32[4,128,128]{2,1,0:T(8,128)}, s32[]{:T(128)}) while((s32[]{:T(128)}, f32[512,512]{1,0:T(8,128)S(1)}, s32[4,2]{0,1:T(2,128)S(1)}, f32[4,128,128]{2,1,0:T(8,128)}, s32[]{:T(128)}) %tuple.135), condition=%wide.while_cond.1, body=%wide.while_body.1.sunk | while | flops 2 | bytes 132205 | solution.py:38
  95.9 2.0 bitcast_dynamic-update-slice_fusion.11
  98.6 2.0 bitcast_dynamic-update-slice_fusion.11
  101.2 2.0 bitcast_dynamic-update-slice_fusion.11
  103.8 2.0 bitcast_dynamic-update-slice_fusion.11
  105.8 40.1 %custom-call.38 = f32[4,128,128]{1,2,0:T(8,128)S(1)} custom-call(f32[4,128,128]{2,1,0:T(8,128)} %get-tuple-element.79), custom_call_target="InvertDiagBlocksLowerTriangular" | custom-call | tf_op jit(solution)/shard_map/cond/branch_1_fun/triangular_solve/custom-call.3 | solution.py:38
  154.1 1.9 broadcast_select_fusion.3
  158.0 92.5 %all-reduce.8.cloned.1.call-done = (f32[512,256]{0,1:T(8,128)}, f32[512,512]{1,0:T(8,128)}) async-done(((f32[512,256]{0,1:T(8,128)}, f32[512,512]{1,0:T(8,128)}), (f32[512,256]{0,1:T(8,128)}, f32[512,512]{1,0:T(8,128)})) %all-reduce.8.cloned.1.call-update) | async-done | bytes 1572880 | tf_op jit(solution)/shard_map/psum | solution.py:17
  250.5 1.3 fusion.103
  251.9 8.0 %while.9 = (s32[]{:T(128)}, f32[512,512]{1,0:T(8,128)S(1)}, s32[4,2]{0,1:T(2,128)S(1)}, f32[4,128,128]{2,1,0:T(8,128)S(1)}, s32[]{:T(128)}) while((s32[]{:T(128)}, f32[512,512]{1,0:T(8,128)S(1)}, s32[4,2]{0,1:T(2,128)S(1)}, f32[4,128,128]{2,1,0:T(8,128)S(1)}, s32[]{:T(128)}) %tuple.140), condition=%wide.while_cond.2, body=%wide.while_body.2.sunk | while | flops 2 | bytes 131189 | solution.py:38
  252.5 1.4 bitcast_dynamic-update-slice_fusion.8
  254.5 1.4 bitcast_dynamic-update-slice_fusion.8
  256.5 1.4 bitcast_dynamic-update-slice_fusion.8
  258.5 1.4 bitcast_dynamic-update-slice_fusion.8
  259.9 39.3 %custom-call.29 = f32[4,128,128]{1,2,0:T(8,128)S(1)} custom-call(f32[4,128,128]{2,1,0:T(8,128)S(1)} %get-tuple-element.64), custom_call_target="InvertDiagBlocksLowerTriangular" | custom-call | tf_op jit(solution)/shard_map/triangular_solve | solution.py:38
  301.5 1.8 convolution_subtract_fusion.15
  304.0 2.7 fusion.96
  307.4 1.5 bitcast_bitcast_fusion
  309.7 10.4 %conditional.3 = (f32[512,512]{1,0:T(8,128)}, f32[512,128]{1,0:T(8,128)}, f32[512,128]{1,0:T(8,128)S(1)}, f32[512,256]{0,1:T(8,128)}) conditional(s32[]{:T(128)} %convert_element_type.69, () %tuple.32, (s32[2,3,512]{2,0,1:T(2,128)S(1)}, f32[8,512,128]{2,1,0:T(8,128)}, bf16[8,512,128]{2,1,0:T(8,128)(2,1)S(1)}, s32[8,512]{1,0:T(8,128)S(1)}, ...), branch_computations={%region_12.15_spmd, %region_13.16_spmd} | conditional | flops 1919715328 | bytes 30088544 | solution.py:115
  324.3 1.5 convert_multiply_fusion
  326.0 2.0 fusion.109
  328.0 3.8 fusion.134
  331.8 234.4 %all-reduce.6.cloned.1.call-done = (f32[512,128]{1,0:T(8,128)}, f32[512,128]{1,0:T(8,128)}, f32[512,512]{1,0:T(8,128)}, f32[512,256]{0,1:T(8,128)}) async-done(((f32[512,128]{1,0:T(8,128)}, f32[512,128]{1,0:T(8,128)}, f32[512,512]{1,0:T(8,128)}, f32[512,256]{0,1:T(8,128)}), (f32[512,128]{1,0:T(8,128)}, f32[512,128]{1,0:T(8,128)}, f32[512,512]{1,0:T(8,128)}, ...) | async-done | bytes 2097168 | tf_op jit(solution)/shard_map/psum | solution.py:17
  566.3 5.6 convolution_bitcast_fusion.1
  572.0 8.2 %while.10 = (s32[]{:T(128)}, f32[512,512]{1,0:T(8,128)S(1)}, s32[4,2]{0,1:T(2,128)S(1)}, f32[4,128,128]{2,1,0:T(8,128)S(1)}, s32[]{:T(128)}) while((s32[]{:T(128)}, f32[512,512]{1,0:T(8,128)S(1)}, s32[4,2]{0,1:T(2,128)S(1)}, f32[4,128,128]{2,1,0:T(8,128)S(1)}, s32[]{:T(128)}) %tuple.156), condition=%wide.while_cond.3, body=%wide.while_body.3.sunk | while | flops 2 | bytes 131189 | solution.py:38
  572.7 1.4 bitcast_dynamic-update-slice_fusion.9
  574.8 1.4 bitcast_dynamic-update-slice_fusion.9
  576.8 1.4 bitcast_dynamic-update-slice_fusion.9
  578.9 1.4 bitcast_dynamic-update-slice_fusion.9
  580.9 40.3 %custom-call.30 = f32[4,128,128]{1,2,0:T(8,128)S(1)} custom-call(f32[4,128,128]{2,1,0:T(8,128)} %copy-done.22), custom_call_target="InvertDiagBlocksLowerTriangular" | custom-call | tf_op jit(solution)/shard_map/triangular_solve | solution.py:38
  621.2 2.9 negate_bitcast_fusion
  626.2 1.8 convolution_subtract_fusion.14
  629.1 3.5 convolution_subtract_fusion.13
  633.7 5.5 fusion.80
  640.9 2.0 copy.46
  642.9 7.8 %fusion.72 = f32[8,256,256]{2,1,0:T(8,128)S(1)} fusion(f32[8,512,256]{2,0,1:T(8,128)S(1)} %bitcast.272, f32[512,256]{0,1:T(8,128)S(1)} %copy-done.17), kind=kOutput, calls=%fused_computation.162 | convolution fusion | flops 3221225472 | bytes 6815744 | tf_op jit(solution)/shard_map/nbk,bc->nkc/dot_general | solution.py:73
  650.7 2.6 fusion.71
  653.3 1.9 copy.112
  656.2 5.5 copy.35
  661.7 1.5 pad_maximum_fusion.3
  (144 shorter events, 45.4 us)
Async XLA Ops:
  7.2 243.3 %all-reduce.8.cloned.1.call-start = ((), (), s32[]{:S(2)}) async-start(), calls=%async_computation.1 | async-start | bytes 3145728 | tf_op jit(solution)/shard_map/psum | solution.py:17
  153.0 3.1 copy-start.24
  153.0 3.1 copy-start.20
  156.0 410.3 %all-reduce.6.cloned.1.call-start = ((), (), s32[]{:S(2)}) async-start(), calls=%async_computation | async-start | bytes 4194304 | tf_op jit(solution)/shard_map/psum | solution.py:17
  300.9 3.1 copy-start.18
  304.0 4.9 copy-start.6
  307.4 1.5 copy-start.15
  307.4 2.0 copy-start.3
  307.4 2.3 copy-start.12
  307.4 2.3 copy-start.23
  321.2 1.8 copy-start.21
  324.3 1.6 copy-start.7
  324.3 1.6 copy-start.13
  324.3 1.7 copy-start.16
  326.0 2.0 copy-start.4
  566.3 5.6 copy-start.9
  580.2 0.7 copy-start.22
  640.9 2.0 copy-start.17
  642.9 7.8 %copy-start = (f32[8,256,512]{2,1,0:T(8,128)S(1)}, f32[8,256,512]{2,1,0:T(8,128)}, u32[]{:S(2)}) copy-start(f32[8,256,512]{2,1,0:T(8,128)} %fusion.134) | copy-start | bytes 12582916
  642.9 7.8 %copy-start.5 = (bf16[8,1,512,128]{3,2,1,0:T(8,128)(2,1)S(1)}, bf16[8,1,512,128]{3,2,1,0:T(8,128)(2,1)}, u32[]{:S(2)}) copy-start(bf16[8,1,512,128]{3,2,1,0:T(8,128)(2,1)} %param.19) | copy-start | bytes 3145732
  642.9 7.8 %copy-start.19 = (bf16[8,1,512,128]{3,2,1,0:T(8,128)(2,1)S(1)}, bf16[8,1,512,128]{3,2,1,0:T(8,128)(2,1)}, u32[]{:S(2)}) copy-start(bf16[8,1,512,128]{3,2,1,0:T(8,128)(2,1)} %param.21) | copy-start | bytes 3145732
  653.3 2.0 copy-start.14
  656.2 5.5 copy-start.8
  656.2 5.5 copy-start.10
Sparse Core Ops, SparseCore 0:
  156.1 94.3 all-reduce.7
  323.0 243.1 all-reduce.5
where the time goes:
time: 680 us; the launch traced here: 670 us
  waiting for transfers between devices  327 us (48%)
  other arithmetic  215 us (32%)
  matrix products  55.6 us (8%)
  local copies, waits for them, and re-layouts  46.8 us (7%)
  between operations  15 us (2%)
  loops' own time  10.8 us (2%)
    psum x2, waiting for transfers between devices, spread(): return lax.psum(jnp.where(mine, shard, jnp.zeros_like(shard)), axis)  327 us
    another operation x11, other arithmetic, triangular(): lax.linalg.triangular_solve(lower, target, left_side=True, lower=True)  122 us
    another operation x14, other arithmetic, first_factor(): lower = jnp.linalg.cholesky(kernel_tile(coords[0]))  78.8 us
    another operation x21, matrix products, triangular(): lax.linalg.triangular_solve(lower, target, left_side=True, lower=True)  29 us
    another operation x29, local copies, waits for them, and re-layouts  19.5 us
    unnamed x52, local copies, waits for them, and re-layouts  13.7 us
  transfers between devices with their start and end apart: 2, of which 2 were waited for; matrix products, arithmetic and copies ran while one was open for 2% of the time, Pallas kernels for 0%

commit v1 on v0

v1 whole, which is shorter than its diff:
```python
import functools
import math

import jax
import jax.numpy as jnp
from jax import lax
from jax.experimental import pallas as pl
from jax.experimental.pallas import tpu as pltpu
from jax.sharding import PartitionSpec as P

NRHS = 256
LANES = 128
SUB = 8
f32 = jnp.float32
bf16 = jnp.bfloat16
highest = lax.Precision.HIGHEST
VMEM = pltpu.VMEM


def nn(left, right):
    return jnp.dot(left, right, precision=highest, preferred_element_type=f32)


def tn(left, right):
    return lax.dot_general(
        left, right, (((0,), (0,)), ((), ())), precision=highest, preferred_element_type=f32
    )


def nt(left, right):
    return lax.dot_general(
        left, right, (((1,), (1,)), ((), ())), precision=highest, preferred_element_type=f32
    )


def parts_of(value, number):
    pieces = []
    for _ in range(number):
        piece = value.astype(bf16)
        pieces.append(piece)
        value = value - piece.astype(f32)
    return pieces


def exact_dot(left, right, dims):
    return lax.dot_general(left, right, (dims, ((), ())), preferred_element_type=f32)


def row_of(value, index):
    return jnp.broadcast_to(value[index : index + 1, :], value.shape)


def column_of(value, index):
    return jnp.broadcast_to(value[:, index : index + 1], value.shape)


def factor_block(rows, put):
    number = len(rows)
    lane = lax.broadcasted_iota(jnp.int32, (SUB, LANES), 1)
    sub = lax.broadcasted_iota(jnp.int32, (SUB, LANES), 0)
    for step in range(number):
        low = SUB * step
        here = (lane >= low) & (lane < low + SUB)
        columns = [[column_of(rows[i], low + c) for c in range(SUB)] for i in range(step, number)]
        pivot = list(columns[0])
        plain = rows[step]
        work = jnp.where(here, jnp.where(lane - low == sub, 1.0, 0.0).astype(f32), plain)
        upper = jnp.zeros((SUB, LANES), f32)
        inverse = jnp.zeros((SUB, LANES), f32)
        for first in range(0, SUB, 2):
            second = first + 1
            left, right = pivot[first], pivot[second]
            a, b, c = row_of(left, first), row_of(left, second), row_of(right, second)
            scale = 1.0 / (a * c - b * b)
            is_first, is_second = sub == first, sub == second
            both = is_first | is_second
            m_first = jnp.where(is_first, -c, jnp.where(is_second, b, left * c - right * b)) * scale
            m_second = jnp.where(is_first, b, jnp.where(is_second, -a, right * a - left * b)) * scale

            def eliminate(value, top, bottom):
                return jnp.where(both, 0.0, value) - m_first * top - m_second * bottom

            w_top, w_bottom = row_of(work, first), row_of(work, second)
            p_top, p_bottom = row_of(plain, first), row_of(plain, second)
            root = lax.rsqrt(a)
            below = b * root
            last = lax.rsqrt(c - below * below)
            upper = jnp.where(
                is_first,
                p_top * root,
                jnp.where(is_second, (p_bottom - below * (p_top * root)) * last, upper),
            )
            inverse = jnp.where(
                is_first,
                w_top * root,
                jnp.where(is_second, (w_bottom - below * (w_top * root)) * last, inverse),
            )
            for other in range(second + 1, SUB):
                pivot[other] = eliminate(
                    pivot[other], row_of(pivot[other], first), row_of(pivot[other], second)
                )
            work = eliminate(work, w_top, w_bottom)
            if second < SUB - 1:
                plain = eliminate(plain, p_top, p_bottom)
        put(step, jnp.where(lane - low >= sub, upper, 0.0), jnp.where(lane - low <= sub, inverse, 0.0))
        solved = [row_of(work, c) for c in range(SUB)]
        for i in range(step + 1, number):
            terms = [columns[i - step][c] * solved[c] for c in range(SUB)]
            while len(terms) > 1:
                terms = [terms[k] + terms[k + 1] for k in range(0, len(terms), 2)]
            rows[i] = jnp.where(here, 0.0, rows[i]) - terms[0]


def factor_tile(matrix, upper, inverse):
    size = matrix.shape[0]
    blocks = size // LANES
    for k in range(blocks):
        low, high = LANES * k, LANES * (k + 1)

        def put(step, upper_rows, inverse_rows):
            at = pl.ds(low + SUB * step, SUB)
            upper[at, low:high] = upper_rows
            inverse[at, low:high] = inverse_rows

        factor_block(
            [matrix[low + SUB * i : low + SUB * (i + 1), low:high] for i in range(LANES // SUB)], put
        )
        corner = inverse[low:high, low:high]
        if k > 0:
            inverse[low:high, :low] = nn(corner, matrix[low:high, :low])
            upper[low:high, :low] = jnp.zeros((LANES, low), f32)
        if k < blocks - 1:
            panel = nn(corner, matrix[low:high, high:])
            upper[low:high, high:] = panel
            inverse[low:high, high:] = jnp.zeros((LANES, size - high), f32)
            matrix[high:, high:] = matrix[high:, high:] - tn(panel, panel)
            if k > 0:
                matrix[high:, :low] = matrix[high:, :low] - tn(panel, inverse[low:high, :low])
            matrix[high:, low:high] = -tn(panel, corner)


def kernel_tile(points):
    size = points.shape[1]
    spots = points.astype(f32)
    square = jnp.sum(spots * spots, axis=0, keepdims=True)
    one = jnp.ones_like(square)
    zero = jnp.zeros((11, size), f32)
    left = jnp.concatenate([spots, square, one, zero], axis=0).astype(bf16)
    right = jnp.concatenate([-2.0 * spots, one, square, zero], axis=0).astype(bf16)
    distance = exact_dot(left, right, ((0,), (0,)))
    row = lax.broadcasted_iota(jnp.int32, (size, size), 0)
    column = lax.broadcasted_iota(jnp.int32, (size, size), 1)
    return lax.rsqrt(distance + 1.0) * (1.0 / (4.0 * math.pi)) + jnp.where(row == column, 1.0, 0.0)


def onehot_rows(label_row):
    size = label_row.shape[1]
    row = lax.broadcasted_iota(jnp.int32, (NRHS, size), 0).astype(f32)
    return jnp.where(row == label_row, 1.0, 0.0).astype(f32)


def store_lower(upper, lower):
    size = upper.shape[0]
    for i in range(0, size, LANES):
        for j in range(0, size, LANES):
            if i >= j:
                lower[i : i + LANES, j : j + LANES] = upper[j : j + LANES, i : i + LANES].T
            else:
                lower[i : i + LANES, j : j + LANES] = jnp.zeros((LANES, LANES), f32)


def first_kernel(coords, diagonal, inverse, matrix, upper, lower, sem):
    matrix[...] = kernel_tile(coords[0])
    factor_tile(matrix, upper, inverse)
    store_lower(upper, lower)
    copy = pltpu.make_async_copy(lower, diagonal.at[0], sem)
    copy.start()
    copy.wait()


def second_kernel(
    coords, shared, inverse, _, diagonal, y_first, y_second, z_first, z_second,
    matrix, upper, lower, last, sem,
):
    size = inverse.shape[0]
    u_one = shared[0:size, :]
    v_one = shared[size : 2 * size, :]
    labels = shared[2 * size : 2 * size + 16, :].astype(f32)
    spread = size // LANES

    def label_row(which):
        return jnp.concatenate(
            [labels[which * spread + i : which * spread + i + 1, :] for i in range(spread)], axis=1
        )

    def two_sided(value_parts, other, dims):
        return sum(exact_dot(piece, other, dims) for piece in reversed(value_parts))

    inverse_parts = parts_of(inverse[...], 3)
    first_b = onehot_rows(label_row(0)).astype(bf16)
    y0 = two_sided(inverse_parts, first_b, ((1,), (1,)))
    y_first[...] = y0
    w_one = two_sided(inverse_parts, v_one, ((1,), (0,)))
    gram = tn(w_one, w_one)
    wide_u = u_one.astype(f32)
    left = nn(wide_u, gram)
    matrix[...] = kernel_tile(coords[1]) - nt(left, wide_u)
    target = onehot_rows(label_row(1)).T - nn(wide_u, tn(w_one, y0))
    z0 = tn(inverse[...], y0)
    p_one = tn(inverse[...], w_one)
    factor_tile(matrix, upper, last)
    store_lower(upper, lower)
    copy = pltpu.make_async_copy(lower, diagonal.at[1], sem)
    copy.start()
    y1 = nn(last[...], target)
    y_second[...] = y1
    z1 = tn(last[...], y1)
    zc = z0 - nn(p_one, tn(wide_u, z1))
    for which, ref in ((zc, z_first), (z1, z_second)):
        big, small = parts_of(which, 2)
        ref[:, :NRHS] = big
        ref[:, NRHS:] = small
    copy.wait()


def tile_kernel(
    position, ranks, labels, u0, v0, u1, v1, y_first, y_second, z_first, z_second, out
):
    step = pl.program_id(0)

    def weights(v, z, rank):
        both = exact_dot(v[...], z[...], ((0,), (0,)))
        value = both[:, :NRHS] + both[:, NRHS:]
        row = lax.broadcasted_iota(jnp.int32, value.shape, 0)
        return jnp.where(row < rank, value, 0.0)

    h = jnp.concatenate(
        [weights(v0, z_first, ranks[step, 0]), weights(v1, z_second, ranks[step, 1])], axis=0
    )
    big, small = parts_of(h, 2)
    u = jnp.concatenate([u0[...], u1[...]], axis=1)
    total = exact_dot(u, big, ((1,), (0,))) + exact_dot(u, small, ((1,), (0,)))
    size = labels.shape[1]
    column = jnp.broadcast_to(labels[...], (LANES, size)).astype(f32).T
    lane = lax.broadcasted_iota(jnp.int32, (size, LANES), 1).astype(f32)
    hot = jnp.concatenate(
        [jnp.where(column == lane + float(LANES * i), 1.0, 0.0) for i in range(NRHS // LANES)], axis=1
    )
    out[...] = hot - total

    @pl.when((step == 0) & (position[0] == 0))
    def _():
        out[...] = y_first[...]

    @pl.when((step == 0) & (position[0] == 1))
    def _():
        out[...] = y_second[...]


def local(coords, labels, ranks, u_first, v_first, u_second, v_second):
    position = lax.axis_index("row")
    cycles, _, size, breadth = u_first.shape
    whole = pl.BlockSpec(memory_space=VMEM)
    anywhere = pl.BlockSpec(memory_space=pl.ANY)
    params = pltpu.CompilerParams(vmem_limit_bytes=56 << 20)

    kept = jnp.arange(breadth, dtype=jnp.int32)[None, :] < ranks[0, 0, 0]
    v_one = jnp.where(kept & (position == 1), v_first[0, 0], 0)
    u_one = jnp.where(position == 1, u_first[0, 0], 0)
    hot = labels[0, 0].astype(bf16).reshape(size // breadth, breadth)
    payload = jnp.concatenate(
        [
            u_one,
            v_one,
            jnp.where(position == 0, hot, 0),
            jnp.where(position == 1, hot, 0),
            jnp.zeros((8, breadth), bf16),
        ],
        axis=0,
    )
    shared = lax.psum(payload, "row")

    square = jax.ShapeDtypeStruct((size, size), f32)
    tall = jax.ShapeDtypeStruct((size, NRHS), f32)
    pair = jax.ShapeDtypeStruct((size, 2 * NRHS), bf16)
    stack = jax.ShapeDtypeStruct((2, size, size), f32)
    room = [pltpu.VMEM((size, size), f32)] * 3
    diagonal, inverse = pl.pallas_call(
        first_kernel,
        out_shape=[stack, square],
        in_specs=[whole],
        out_specs=[anywhere, whole],
        scratch_shapes=room + [pltpu.SemaphoreType.DMA],
        compiler_params=params,
        cost_estimate=pl.CostEstimate(flops=10**9, bytes_accessed=10**8, transcendentals=0),
        name="first",
    )(coords)
    diagonal, y_first, y_second, z_first, z_second = pl.pallas_call(
        second_kernel,
        out_shape=[stack, tall, tall, pair, pair],
        in_specs=[whole, whole, whole, anywhere],
        out_specs=[anywhere, whole, whole, whole, whole],
        scratch_shapes=room + [pltpu.VMEM((size, size), f32), pltpu.SemaphoreType.DMA],
        input_output_aliases={3: 0},
        compiler_params=params,
        name="second",
    )(coords, shared, inverse, diagonal)

    def tile(width):
        return pl.BlockSpec((None, None, size, width), lambda i, *_: (i, 0, 0, 0))

    def fixed(width):
        return pl.BlockSpec((size, width), lambda i, *_: (0, 0))

    eliminated = pl.pallas_call(
        tile_kernel,
        out_shape=jax.ShapeDtypeStruct((cycles, 1, size, NRHS), f32),
        grid_spec=pltpu.PrefetchScalarGridSpec(
            num_scalar_prefetch=2,
            grid=(cycles,),
            in_specs=[pl.BlockSpec((None, 1, size), lambda i, *_: (i, 0, 0))]
            + [tile(breadth)] * 4
            + [fixed(NRHS)] * 2
            + [fixed(2 * NRHS)] * 2,
            out_specs=tile(NRHS),
        ),
        compiler_params=params,
        name="tiles",
    )(
        position.astype(jnp.int32).reshape(1), ranks[:, 0], labels,
        u_first, v_first, u_second, v_second, y_first, y_second, z_first, z_second,
    )
    return (eliminated, diagonal)


def solution(mesh):
    in_specs = (
        P("parts", None, None),
        P("parts", "row", None),
        P("parts", "row", None),
        P("parts", "row", None, None),
        P("parts", "row", None, None),
        P("parts", "row", None, None),
        P("parts", "row", None, None),
    )
    out_specs = (P("parts", "row", None, None), P("parts", None, None))
    return jax.shard_map(local, mesh=mesh, in_specs=in_specs, out_specs=out_specs, check_vma=False)
```

time: 680 us -> 156 us (0.23); the launches traced: 670 us -> 156 us
  waiting for transfers between devices: 327 us -> 66.3 us
  other arithmetic: 215 us -> 3.19 us
  Pallas kernels: 0 us -> 65.5 us
  matrix products: 55.6 us -> 0 us
  local copies, waits for them, and re-layouts: 46.8 us -> 6.37 us
  loops' own time: 10.8 us -> 0 us
    psum x2 -> x1, waiting for transfers between devices: 327 us -> 66.3 us  [local(): shared = lax.psum(payload, 'row')]
    another operation x26 -> x0, other arithmetic: 202 us -> none  [the longest x11 122 us: triangular(): lax.linalg.triangular_solve(lower, target, left_side=True, lower=True)]
    pallas_call x0 -> x3, Pallas kernels: none -> 65.5 us  [the longest x1 32.1 us: local(): pl.pallas_call(second_kernel, out_shape=[stack, tall, tall, pair, pair],...]
    another operation x49 -> x0, local copies, waits for them, and re-layouts: 31.8 us -> none
    another operation x27 -> x0, matrix products: 30.9 us -> none  [the longest x21 29 us: triangular(): lax.linalg.triangular_solve(lower, target, left_side=True, lower=True)]
    dot_general x6 -> x0, matrix products: 24.7 us -> none  [the longest x1 7.79 us: update(): jnp.einsum('nbk,bc->nkc', factor, second_sol, precision=highest)]
    unnamed x52 -> x1, local copies, waits for them, and re-layouts: 13.7 us -> 1.31 us
    another operation x5 -> x0, loops' own time: 10.8 us -> none  [the longest x1 7.71 us: local(): lax.cond(position == 1, second_factor, second_empty)]
  transfers between devices with their start and end apart: 2 -> 1, of which waited for: 2 -> 1; matrix products, arithmetic and copies ran while one was open for 2% -> 2% of each run, Pallas kernels for 0% -> 15%
where the time goes in v1:
time: 156 us
  waiting for transfers between devices  66.3 us (42%)
  Pallas kernels  65.5 us (42%)
  between operations  14.1 us (9%)
  local copies, waits for them, and re-layouts  6.37 us (4%)
  other arithmetic  3.19 us (2%)
    psum x1, waiting for transfers between devices, local(): shared = lax.psum(payload, 'row')  66.3 us
    pallas_call x1, Pallas kernels, local(): pl.pallas_call(second_kernel, out_shape=[stack, tall, tall, pair, pair],...  32.1 us
    pallas_call x1, Pallas kernels, local(): pl.pallas_call(first_kernel, out_shape=[stack, square], in_specs=[whole],...  22.9 us
    pallas_call x1, Pallas kernels, local(): pl.pallas_call(tile_kernel, out_shape=jax.ShapeDtypeStruct((cycles, 1, si...  10.6 us
  transfers between devices with their start and end apart: 1, of which 1 were waited for; matrix products, arithmetic and copies ran while one was open for 2% of the time, Pallas kernels for 15%

profile of v1, /device:TPU:0, one launch (start us, length us, event | category | flops | bytes accessed | tf_op | source)
XLA Modules:
  0.0 155.5 jit_solution(17471957046752844533)
XLA Ops:
  7.2 0.0 all-reduce.2.cloned.1.call-start
  7.2 1.2 slice.14
  8.4 0.7 compare_and_fusion
  9.1 0.9 select_bitcast_fusion
  10.0 0.7 fusion.1
  10.7 0.9 bitcast_select_fusion
  11.6 2.5 %concatenate.3 = bf16[1040,128]{1,0:T(8,128)(2,1)} concatenate(bf16[512,128]{1,0:T(8,128)(2,1)S(1)} %select_bitcast_fusion, bf16[512,128]{1,0:T(8,128)(2,1)S(1)} %bitcast_select_fusion, bf16[4,128]{1,0:T(4,128)(2,1)S(1)} %bitcast.10, bf16[4,128]{1,0:T(4,128)(2,1)S(1)} %bitcast.9, bf16[8,128]{1,0:T(8,128)(2,1)S(1)} %broadcast_in_dim.29), dimensions={0} | concatenate | bytes 532480 | tf_op jit(solution)/shard_map/concatenate | solution.py:271
  14.1 0.0 all-reduce.2.cloned.1.call-update
  14.2 1.3 copy.12.ranks
  15.5 1.3 copy.11.coords
  16.8 22.9 %first.1 = (f32[2,512,512]{2,1,0:T(8,128)}, f32[512,512]{1,0:T(8,128)}) custom-call(s32[2,3,512]{2,1,0:T(4,128)} %copy.11.coords), custom_call_target="tpu_custom_call" | custom-call | flops 1000000000 | bytes 100000000 | tf_op jit(solution)/shard_map/first/pallas_call | solution.py:288
  39.7 66.3 %all-reduce.2.cloned.1.call-done.shared = bf16[1040,128]{1,0:T(8,128)(2,1)} async-done(((bf16[1040,128]{1,0:T(8,128)(2,1)}), bf16[1040,128]{1,0:T(8,128)(2,1)}) %all-reduce.2.cloned.1.call-update) | async-done | bytes 266256 | tf_op jit(solution)/shard_map/psum | solution.py:281
  106.0 32.1 %second.1 = (f32[2,512,512]{2,1,0:T(8,128)}, f32[512,256]{1,0:T(8,128)}, f32[512,256]{1,0:T(8,128)}, bf16[512,512]{1,0:T(8,128)(2,1)}, bf16[512,512]{1,0:T(8,128)(2,1)}) custom-call(s32[2,3,512]{2,1,0:T(4,128)} %copy.11.coords, bf16[1040,128]{1,0:T(8,128)(2,1)} %all-reduce.2.cloned.1.call-done.shared, ...), custom_call_target="tpu_custom_call", output_to_operand_aliasing={{0}: (3, {})} | custom-call | tf_op jit(solution)/shard_map/second/pallas_call | solution.py:298
  138.1 10.6 %tiles.1 = f32[8,1,512,256]{3,2,1,0:T(8,128)} custom-call(s32[1]{0:T(128)} %bitcast.position, s32[8,2]{1,0:T(8,128)} %copy.12.ranks, s32[8,1,512]{2,1,0:T(1,128)} %labels.1, bf16[8,1,512,128]{3,2,1,0:T(8,128)(2,1)} %u0.1, bf16[8,1,512,128]{3,2,1,0:T(8,128)(2,1)} %v0.1, bf16[8,1,512,128]{3,2,1,0:T(8,128)(2,1)} %u1_.1, bf16[8,1,512,128]{3,2,1,0:T(8,128)(2,1)} %v1.1, ...), custom_call_target="tpu_custom_call" | custom-call | tf_op jit(solution)/shard_map/tiles/pallas_call | solution.py:315
  (1 shorter events, 0.0 us)
Async XLA Ops:
  7.2 98.8 %all-reduce.2.cloned.1.call-start = ((), (), s32[]{:S(2)}) async-start(), calls=%async_computation | async-start | bytes 532480 | tf_op jit(solution)/shard_map/psum | solution.py:281
Sparse Core Ops, SparseCore 0:
  14.3 91.6 all-reduce.1

commit v2 on v0

v2 whole, which is shorter than its diff:
```python
import functools
import math

import jax
import jax.numpy as jnp
from jax import lax
from jax.experimental import pallas as pl
from jax.experimental.pallas import tpu as pltpu
from jax.sharding import PartitionSpec as P

NRHS = 256
LANES = 128
SUB = 8
HALF = 64
f32 = jnp.float32
bf16 = jnp.bfloat16
highest = lax.Precision.HIGHEST
high = lax.Precision.HIGH
VMEM = pltpu.VMEM
NN, TN, NT = ((1,), (0,)), ((0,), (0,)), ((1,), (1,))


def mul(left, right, dims=NN, precision=None):
    return lax.dot_general(
        left, right, (dims, ((), ())), precision=precision, preferred_element_type=f32
    )


def parts_of(value, number):
    pieces = []
    for _ in range(number):
        piece = value.astype(bf16)
        pieces.append(piece)
        value = value - piece.astype(f32)
    return pieces


def split_left(left, right, dims=NN, number=3):
    return sum(mul(piece, right, dims) for piece in reversed(parts_of(left, number)))


def split_right(left, right, dims=NN, number=3):
    return sum(mul(left, piece, dims) for piece in reversed(parts_of(right, number)))


def row_of(value, index):
    return jnp.broadcast_to(value[index : index + 1, :], value.shape)


def column_of(value, index):
    return jnp.broadcast_to(value[:, index : index + 1], value.shape)


def factor_half(rows, base, put):
    number = len(rows)
    lane = lax.broadcasted_iota(jnp.int32, (SUB, LANES), 1)
    sub = lax.broadcasted_iota(jnp.int32, (SUB, LANES), 0)
    pair = range(2)
    for step in range(0, number, 2):
        low = SUB * (base + step)
        here = (lane >= low) & (lane < low + 2 * SUB)
        columns = [[column_of(rows[i], low + c) for c in range(2 * SUB)] for i in range(step, number)]
        pivot = [list(columns[0]), list(columns[1])]
        plain = [rows[step], rows[step + 1]]
        work = [
            jnp.where(here, jnp.where(lane - low == sub + SUB * g, 1.0, 0.0).astype(f32), plain[g])
            for g in pair
        ]
        upper = [jnp.zeros((SUB, LANES), f32)] * 2
        inverse = [jnp.zeros((SUB, LANES), f32)] * 2
        for first in range(0, 2 * SUB, 2):
            second = first + 1
            home, top, bottom = first // SUB, first % SUB, first % SUB + 1
            left, right = pivot[home][first], pivot[home][second]
            a, b, c = row_of(left, top), row_of(left, bottom), row_of(right, bottom)
            scale = 1.0 / (a * c - b * b)
            is_top, is_bottom = sub == top, sub == bottom
            both = is_top | is_bottom
            m_top, m_bottom = [], []
            for g in pair:
                p = pivot[g][first] * c - pivot[g][second] * b
                q = pivot[g][second] * a - pivot[g][first] * b
                if g == home:
                    p = jnp.where(is_top, -c, jnp.where(is_bottom, b, p))
                    q = jnp.where(is_top, b, jnp.where(is_bottom, -a, q))
                m_top.append(p * scale)
                m_bottom.append(q * scale)

            def eliminate(g, value, above, below):
                kept = jnp.where(both, 0.0, value) if g == home else value
                return kept - m_top[g] * above - m_bottom[g] * below

            w_top, w_bottom = row_of(work[home], top), row_of(work[home], bottom)
            p_top, p_bottom = row_of(plain[home], top), row_of(plain[home], bottom)
            root = lax.rsqrt(a)
            factor = b * root
            last = lax.rsqrt(c - factor * factor)
            upper[home] = jnp.where(
                is_top,
                p_top * root,
                jnp.where(is_bottom, (p_bottom - factor * (p_top * root)) * last, upper[home]),
            )
            inverse[home] = jnp.where(
                is_top,
                w_top * root,
                jnp.where(is_bottom, (w_bottom - factor * (w_top * root)) * last, inverse[home]),
            )
            for other in range(second + 1, 2 * SUB):
                above, below = row_of(pivot[home][other], top), row_of(pivot[home][other], bottom)
                for g in pair:
                    pivot[g][other] = eliminate(g, pivot[g][other], above, below)
            work = [eliminate(g, work[g], w_top, w_bottom) for g in pair]
            plain = [
                eliminate(g, plain[g], p_top, p_bottom) if g >= home else plain[g] for g in pair
            ]
        for g in pair:
            put(
                step + g,
                jnp.where(lane - low >= sub + SUB * g, upper[g], 0.0),
                jnp.where(lane - low <= sub + SUB * g, inverse[g], 0.0),
            )
        if step + 2 < number:
            solved = [row_of(work[c // SUB], c % SUB) for c in range(2 * SUB)]
            for i in range(step + 2, number):
                terms = [columns[i - step][c] * solved[c] for c in range(2 * SUB)]
                while len(terms) > 1:
                    terms = [terms[k] + terms[k + 1] for k in range(0, len(terms), 2)]
                rows[i] = jnp.where(here, 0.0, rows[i]) - terms[0]


def factor_block(rows, put):
    lane = lax.broadcasted_iota(jnp.int32, (SUB, LANES), 1)
    group = HALF // SUB
    for half in range(LANES // HALF):
        done = [None] * group

        def put_half(step, upper_rows, inverse_rows):
            put(group * half + step, upper_rows, inverse_rows)
            done[step] = jnp.where(lane < HALF * (half + 1), inverse_rows, upper_rows)

        chosen = rows[group * half : group * (half + 1)]
        factor_half(chosen, group * half, put_half)
        if half == 0:
            panel = jnp.concatenate(done, axis=0)
            change = mul(panel.T[HALF:], panel, NN, highest)
            for i in range(group):
                rows[group + i] = (
                    jnp.where(lane >= HALF, rows[group + i], 0.0) - change[SUB * i : SUB * (i + 1)]
                )


def factor_step(matrix, strip, corner, panel, k):
    size = matrix.shape[0]
    low, top = LANES * k, LANES * (k + 1)

    def put(step, upper_rows, inverse_rows):
        at = pl.ds(SUB * step, SUB)
        corner[at, :] = upper_rows
        panel[at, low:top] = inverse_rows

    factor_block(
        [matrix[low + SUB * i : low + SUB * (i + 1), low:top] for i in range(LANES // SUB)], put
    )
    own = panel[:, low:top]
    if low:
        strip[:low, :] = jnp.zeros((low, LANES), f32)
        panel[:, :low] = mul(own, matrix[low:top, :low], NN, highest)
        matrix[low:top, :low] = panel[:, :low]
    strip[low:top, :] = corner[...].T
    matrix[low:top, low:top] = own
    if top < size:
        panel[:, top:] = mul(own, matrix[low:top, top:], NN, highest)
        matrix[low:top, top:] = jnp.zeros((LANES, size - top), f32)
        for i in range(top, size, LANES):
            strip[i : i + LANES, :] = panel[:, i : i + LANES].T
        matrix[top:, low:top] = jnp.zeros((size - top, LANES), f32)
        matrix[top:, :] = matrix[top:, :] - mul(strip[top:, :], panel[...], NN, highest)


def kernel_tile(points):
    size = points.shape[1]
    spots = points.astype(f32)
    square = jnp.sum(spots * spots, axis=0, keepdims=True)
    one = jnp.ones_like(square)
    zero = jnp.zeros((11, size), f32)
    left = jnp.concatenate([spots, square, one, zero], axis=0).astype(bf16)
    right = jnp.concatenate([-2.0 * spots, one, square, zero], axis=0).astype(bf16)
    distance = mul(left, right, TN)
    row = lax.broadcasted_iota(jnp.int32, (size, size), 0)
    column = lax.broadcasted_iota(jnp.int32, (size, size), 1)
    return lax.rsqrt(distance + 1.0) * (1.0 / (4.0 * math.pi)) + jnp.where(row == column, 1.0, 0.0)


def onehot_rows(label_row):
    size = label_row.shape[1]
    row = lax.broadcasted_iota(jnp.int32, (NRHS, size), 0).astype(f32)
    return jnp.where(row == label_row, 1.0, 0.0).astype(f32)


def pack_kernel(ranks, labels, u, v, packed):
    size, breadth = u.shape
    position = lax.axis_index("row")
    lane = lax.broadcasted_iota(jnp.int32, (size, breadth), 1)
    own = position == 1
    packed[0:size, :] = jnp.where(own, u[...], 0).astype(bf16)
    packed[size : 2 * size, :] = jnp.where(own & (lane < ranks[0, 0]), v[...], 0).astype(bf16)
    spread = size // breadth
    label = jnp.concatenate(
        [labels[:, breadth * i : breadth * (i + 1)].astype(f32) for i in range(spread)] * 2
        + [jnp.zeros((16 - 2 * spread, breadth), f32)],
        axis=0,
    )
    row = lax.broadcasted_iota(jnp.int32, label.shape, 0)
    source = jnp.where(row < spread, 0, 1)
    packed[2 * size :, :] = jnp.where(source == position, label, 0.0).astype(bf16)


def first_kernel(k, *refs):
    if k == 0:
        coords, matrix, diagonal, strip, corner, panel, sem = refs
        matrix[...] = kernel_tile(coords[:, 0, :])
    else:
        old, _, matrix, diagonal, strip, corner, panel, sem = refs
        matrix[...] = old[...]
    factor_step(matrix, strip, corner, panel, k)
    copy = pltpu.make_async_copy(strip, diagonal.at[0, :, pl.ds(LANES * k, LANES)], sem)
    copy.start()
    copy.wait()


def second_kernel(
    coords, ranks, label_rows, got, came, inverse, u_first, v_first, u_second, v_second, _,
    diagonal, out,
    matrix, strip, corner, panel, y_first, y_second, z_first, z_second, result,
    u0, v0, u1, v1, in_sems, out_sems, strip_sems,
):
    size = inverse.shape[0]
    cycles = result.shape[0]
    loads = [
        pltpu.make_async_copy(source.at[:, 0], target, in_sems.at[i])
        for i, (source, target) in enumerate(
            ((u_first, u0), (v_first, v0), (u_second, u1), (v_second, v1))
        )
    ]
    for load in loads:
        load.start()
    shared = (got[...].astype(f32) + came[...].astype(f32))
    u_one = shared[0:size, :].astype(bf16)
    v_one = shared[size : 2 * size, :].astype(bf16)
    labels = shared[2 * size :, :]
    spread = size // LANES

    def label_row(which):
        return jnp.concatenate(
            [labels[which * spread + i : which * spread + i + 1, :] for i in range(spread)], axis=1
        )

    first_b = onehot_rows(label_row(0)).astype(bf16)
    y0 = split_left(inverse[...], first_b, NT)
    y_first[...] = y0
    w_one = split_left(inverse[...], v_one)
    gram = mul(w_one, w_one, TN, highest)
    left = split_right(u_one, gram)
    matrix[...] = kernel_tile(coords[:, 1, :]) - split_left(left, u_one, NT)
    target = onehot_rows(label_row(1)).T - split_right(u_one, mul(w_one, y0, TN, highest))
    z0 = mul(y0, inverse[...], TN, high)
    p_one = mul(inverse[...], w_one, TN, high)
    strips = []
    for k in range(size // LANES):
        factor_step(matrix, strip.at[k], corner, panel, k)
        copy = pltpu.make_async_copy(
            strip.at[k], diagonal.at[1, :, pl.ds(LANES * k, LANES)], strip_sems.at[k]
        )
        copy.start()
        strips.append(copy)
    y1 = mul(matrix[...], target, NN, high)
    y_second[...] = y1
    z1 = mul(y1, matrix[...], TN, high)
    q_one = split_left(z1, u_one, NN, 2)
    zc = z0 - mul(q_one, p_one, NT, high)
    for which, ref in ((zc, z_first), (z1, z_second)):
        big, small = parts_of(which, 2)
        ref[0:NRHS, :] = big
        ref[NRHS:, :] = small
    for load in loads:
        load.wait()
    columns = label_rows[:, 0, :].astype(f32).T
    lane = lax.broadcasted_iota(jnp.int32, (size, LANES), 1).astype(f32)
    keep = lax.broadcasted_iota(jnp.int32, (NRHS, LANES), 1)
    position = lax.axis_index("row")
    stores = []
    for at in range(0, cycles, 2):
        tiles = range(at, min(at + 2, cycles))

        def weights(v, z, which):
            both = mul(z[...], jnp.concatenate([v[t] for t in tiles], axis=1))
            value = both[:NRHS] + both[NRHS:]
            return [
                jnp.where(keep < ranks[which, t], value[:, LANES * i : LANES * (i + 1)], 0.0)
                for i, t in enumerate(tiles)
            ]

        h_first, h_second = weights(v0, z_first, 0), weights(v1, z_second, 1)
        for i, t in enumerate(tiles):
            both = jnp.concatenate([h_first[i], h_second[i]], axis=1)
            total = split_right(jnp.concatenate([u0[t], u1[t]], axis=1), both, NT, 2)
            column = jnp.broadcast_to(columns[:, t : t + 1], (size, LANES))
            hot = jnp.concatenate(
                [jnp.where(column == lane + float(LANES * j), 1.0, 0.0) for j in range(NRHS // LANES)],
                axis=1,
            )
            result[t] = hot - total
            if t == 0:

                @pl.when(position == 0)
                def _():
                    result[0] = y_first[...]

                @pl.when(position == 1)
                def _():
                    result[0] = y_second[...]

            store = pltpu.make_async_copy(result.at[t], out.at[t, 0], out_sems.at[t])
            store.start()
            stores.append(store)
    for copy in strips + stores:
        copy.wait()


def hops(number):
    chips = number // 2
    strides = [1 << b for b in range(max(chips - 1, 0).bit_length())]
    odd = strides[::-1]
    even = strides[:1] + strides[:0:-1]
    have = {0: [0], 1: [0]}
    result = []
    for index in range(len(strides)):
        pairs = []
        for core, order in ((1, odd), (0, even)):
            new = [(c, c ^ order[index]) for c in have[core] if c ^ order[index] < chips]
            pairs += [(2 * a + core, 2 * b + core) for a, b in new]
            have[core] = have[core] + [b for _, b in new]
        result.append(pairs)
    return result + [[(i, i ^ 1) for i in range(number)]]


def local(row_size, coords, labels, ranks, u_first, v_first, u_second, v_second):
    cycles, _, size, breadth = u_first.shape
    blocks = size // LANES
    whole = pl.BlockSpec(memory_space=VMEM)
    scalars = pl.BlockSpec(memory_space=pltpu.SMEM)
    anywhere = pl.BlockSpec(memory_space=pl.ANY)
    points = jnp.transpose(coords, (1, 0, 2))
    rank_rows = jnp.transpose(ranks, (1, 2, 0))[0]

    packed_size = 2 * size + 16

    def one(width):
        return pl.BlockSpec((None, None, size, width), lambda i: (0, 0, 0, 0))

    packed = pl.pallas_call(
        pack_kernel,
        out_shape=jax.ShapeDtypeStruct((packed_size, breadth), bf16),
        grid=(1,),
        in_specs=[scalars, pl.BlockSpec((None, 1, size), lambda i: (0, 0, 0)), one(breadth), one(breadth)],
        out_specs=pl.BlockSpec((packed_size, breadth), lambda i: (0, 0)),
        compiler_params=pltpu.CompilerParams(vmem_limit_bytes=8 << 20),
        name="pack",
    )(rank_rows, labels, u_first, v_first)

    square = jax.ShapeDtypeStruct((size, size), f32)
    stack = jax.ShapeDtypeStruct((2, size, size), f32)
    room = [
        pltpu.VMEM((LANES, LANES), f32),
        pltpu.VMEM((LANES, size), f32),
    ]
    state = (points,)
    for k in range(blocks):
        state = pl.pallas_call(
            functools.partial(first_kernel, k),
            out_shape=[square, stack],
            in_specs=[whole] if k == 0 else [whole, anywhere],
            out_specs=[whole, anywhere],
            input_output_aliases={} if k == 0 else {0: 0, 1: 1},
            scratch_shapes=[pltpu.VMEM((size, LANES), f32)] + room + [pltpu.SemaphoreType.DMA],
            compiler_params=pltpu.CompilerParams(vmem_limit_bytes=12 << 20),
            cost_estimate=pl.CostEstimate(flops=4 * 10**9, bytes_accessed=10**6, transcendentals=0),
            name=f"first{k}",
        )(*state)
    inverse, diagonal = state

    got = packed
    pairs = hops(row_size)
    for pair in pairs[:-1]:
        got = got + lax.ppermute(got, "row", pair)
    came = lax.ppermute(got, "row", pairs[-1])

    slab = pltpu.VMEM((cycles, size, breadth), bf16)
    diagonal, eliminated = pl.pallas_call(
        second_kernel,
        out_shape=[stack, jax.ShapeDtypeStruct((cycles, 1, size, NRHS), f32)],
        in_specs=[whole, scalars, whole, whole, whole, whole] + [anywhere] * 5,
        out_specs=[anywhere, anywhere],
        scratch_shapes=[
            pltpu.VMEM((size, size), f32),
            pltpu.VMEM((blocks, size, LANES), f32),
            *room,
            pltpu.VMEM((size, NRHS), f32),
            pltpu.VMEM((size, NRHS), f32),
            pltpu.VMEM((2 * NRHS, size), bf16),
            pltpu.VMEM((2 * NRHS, size), bf16),
            pltpu.VMEM((cycles, size, NRHS), f32),
            slab, slab, slab, slab,
            pltpu.SemaphoreType.DMA((4,)),
            pltpu.SemaphoreType.DMA((cycles,)),
            pltpu.SemaphoreType.DMA((blocks,)),
        ],
        input_output_aliases={10: 0},
        compiler_params=pltpu.CompilerParams(vmem_limit_bytes=40 << 20),
        name="second",
    )(
        points, rank_rows, labels, got, came, inverse,
        u_first, v_first, u_second, v_second, diagonal,
    )
    return (eliminated, diagonal)


def solution(mesh):
    in_specs = (
        P("parts", None, None),
        P("parts", "row", None),
        P("parts", "row", None),
        P("parts", "row", None, None),
        P("parts", "row", None, None),
        P("parts", "row", None, None),
        P("parts", "row", None, None),
    )
    out_specs = (P("parts", "row", None, None), P("parts", None, None))
    return jax.shard_map(
        functools.partial(local, mesh.shape["row"]),
        mesh=mesh, in_specs=in_specs, out_specs=out_specs, check_vma=False,
    )
```

time: 680 us -> 61.1 us (0.09); the launches traced: 670 us -> 60.8 us
  waiting for transfers between devices: 327 us -> 1.38 us
  other arithmetic: 215 us -> 0.22 us
  matrix products: 55.6 us -> 0 us
  Pallas kernels: 0 us -> 46.1 us
  local copies, waits for them, and re-layouts: 46.8 us -> 3.88 us
  between operations: 15 us -> 1.06 us
  loops' own time: 10.8 us -> 0 us
  starting transfers between devices: 0.08 us -> 8.18 us
    psum x2 -> x0, waiting for transfers between devices: 327 us -> none  [spread(): return lax.psum(jnp.where(mine, shard, jnp.zeros_like(shard)), axis)]
    another operation x26 -> x0, other arithmetic: 202 us -> none  [the longest x11 122 us: triangular(): lax.linalg.triangular_solve(lower, target, left_side=True, lower=True)]
    pallas_call x0 -> x6, Pallas kernels: none -> 46.1 us  [the longest x1 26.5 us: local(): pl.pallas_call(second_kernel, out_shape=[stack, jax.ShapeDtypeStruct((cyc...]
    another operation x49 -> x0, local copies, waits for them, and re-layouts: 31.8 us -> none
    another operation x27 -> x0, matrix products: 30.9 us -> none  [the longest x21 29 us: triangular(): lax.linalg.triangular_solve(lower, target, left_side=True, lower=True)]
    dot_general x6 -> x0, matrix products: 24.7 us -> none  [the longest x1 7.79 us: update(): jnp.einsum('nbk,bc->nkc', factor, second_sol, precision=highest)]
    another operation x5 -> x0, loops' own time: 10.8 us -> none  [the longest x1 7.71 us: local(): lax.cond(position == 1, second_factor, second_empty)]
    unnamed x52 -> x22, local copies, waits for them, and re-layouts: 13.7 us -> 3.88 us
  transfers between devices with their start and end apart: 2 -> 4, of which waited for: 2 -> 1; matrix products, arithmetic and copies ran while one was open for 2% -> 0% of each run, Pallas kernels for 0% -> 31%
where the time goes in v2:
time: 61.1 us; the launch traced here: 60.8 us
  Pallas kernels  46.1 us (75%)
  starting transfers between devices  8.18 us (13%)
  local copies, waits for them, and re-layouts  3.88 us (6%)
  waiting for transfers between devices  1.38 us (2%)
  between operations  1.06 us (2%)
    pallas_call x1, Pallas kernels, local(): pl.pallas_call(second_kernel, out_shape=[stack, jax.ShapeDtypeStruct((cyc...  26.5 us
    pallas_call x4, Pallas kernels, local(): pl.pallas_call(functools.partial(first_kernel, k), out_shape=[square, sta...  18.9 us
    ppermute x3, starting transfers between devices, local(): got = got + lax.ppermute(got, 'row', pair)  8.11 us
    unnamed x22, local copies, waits for them, and re-layouts  3.88 us
    ppermute x3, waiting for transfers between devices, local(): got = got + lax.ppermute(got, 'row', pair)  1.38 us
  transfers between devices with their start and end apart: 4, of which 1 were waited for; matrix products, arithmetic and copies ran while one was open for 0% of the time, Pallas kernels for 31%

profile of v2, /device:TPU:0, one launch (start us, length us, event | category | flops | bytes accessed | tf_op | source)
XLA Modules:
  0.0 60.8 jit_solution(12849615227318145525)
XLA Ops:
  0.6 0.0 copy-start
  0.6 1.2 %copy-done = bf16[8,1,512,128]{3,2,1,0:T(8,128)(2,1)S(1)} copy-done((bf16[8,1,512,128]{3,2,1,0:T(8,128)(2,1)S(1)}, bf16[8,1,512,128]{3,2,1,0:T(8,128)(2,1)}, u32[]{:S(2)}) %copy-start) | copy-done | bytes 1048600
  1.9 0.0 copy-start.2
  1.9 1.2 %copy-done.2 = bf16[8,1,512,128]{3,2,1,0:T(8,128)(2,1)S(1)} copy-done((bf16[8,1,512,128]{3,2,1,0:T(8,128)(2,1)S(1)}, bf16[8,1,512,128]{3,2,1,0:T(8,128)(2,1)}, u32[]{:S(2)}) %copy-start.2) | copy-done | bytes 1048600
  3.1 0.0 copy-start.6
  3.1 0.7 %copy-done.6 = s32[8,1,512]{2,1,0:T(1,128)S(1)} copy-done((s32[8,1,512]{2,1,0:T(1,128)S(1)}, s32[8,1,512]{2,1,0:T(1,128)}, u32[]{:S(2)}) %copy-start.6) | copy-done | bytes 16408
  3.8 0.0 copy-start.9
  3.8 0.7 %copy-done.9 = s32[8,1,2]{0,2,1:T(2,128)S(1)} copy-done((s32[8,1,2]{0,2,1:T(2,128)S(1)}, s32[8,1,2]{0,2,1:T(2,128)}, u32[]{:S(2)}) %copy-start.9) | copy-done | bytes 88
  4.5 0.0 copy-start.8
  4.5 0.6 %pack.1 = bf16[1040,128]{1,0:T(8,128)(2,1)S(1)} custom-call(s32[2,8]{1,0:T(2,128)S(1)} %bitcast.6, s32[8,1,512]{2,1,0:T(1,128)S(1)} %copy-done.6, bf16[8,1,512,128]{3,2,1,0:T(8,128)(2,1)S(1)} %copy-done, bf16[8,1,512,128]{3,2,1,0:T(8,128)(2,1)S(1)} %copy-done.2), custom_call_target="tpu_custom_call" | custom-call | tf_op jit(solution)/shard_map/pack/pallas_call | solution.py:361
  5.1 4.9 %collective-permute-start = (bf16[1040,128]{1,0:T(8,128)(2,1)S(1)}, bf16[1040,128]{1,0:T(8,128)(2,1)S(1)}, u32[]{:S(2)}, u32[]{:S(2)}) collective-permute-start(bf16[1040,128]{1,0:T(8,128)(2,1)S(1)} %pack.1), channel_id=1, source_target_pairs={{1,9},{0,2},{17,25},{16,18}} | collective-permute-start | bytes 798728 | tf_op jit(solution)/shard_map/ppermute | solution.py:395
  10.0 0.0 copy-done.8
  10.0 5.2 %first0.1 = (f32[512,512]{1,0:T(8,128)S(1)}, f32[2,512,512]{2,1,0:T(8,128)}) custom-call(s32[3,2,512]{2,1,0:T(2,128)S(1)} %bitcast.4), custom_call_target="tpu_custom_call" | custom-call | flops 4000000000 | bytes 1000000 | tf_op jit(solution)/shard_map/first0/pallas_call | solution.py:379
  15.2 0.0 collective-permute-done
  15.2 0.1 add.9
  15.3 1.7 %collective-permute-start.1 = (bf16[1040,128]{1,0:T(8,128)(2,1)S(1)}, bf16[1040,128]{1,0:T(8,128)(2,1)S(1)}, u32[]{:S(2)}, u32[]{:S(2)}) collective-permute-start(bf16[1040,128]{1,0:T(8,128)(2,1)S(1)} %add.9), channel_id=1, source_target_pairs={{1,5},{9,13},{0,8},{2,10},{17,21},{25,29},{16,24},{18,26}} | collective-permute-start | bytes 798728 | tf_op jit(solution)/shard_map/ppermute | solution.py:395
  17.1 4.9 %first1.1 = (f32[512,512]{1,0:T(8,128)S(1)}, f32[2,512,512]{2,1,0:T(8,128)}) custom-call(f32[512,512]{1,0:T(8,128)S(1)} %get-tuple-element.12.refs_0_, f32[2,512,512]{2,1,0:T(8,128)} %get-tuple-element.13.refs_1_), custom_call_target="tpu_custom_call", output_to_operand_aliasing={{0}: (0, {}), {1}: (1, {})} | custom-call | flops 4000000000 | bytes 1000000 | tf_op jit(solution)/shard_map/first1/pallas_call | solution.py:379
  21.9 1.4 %collective-permute-done.1 = bf16[1040,128]{1,0:T(8,128)(2,1)S(1)} collective-permute-done((bf16[1040,128]{1,0:T(8,128)(2,1)S(1)}, bf16[1040,128]{1,0:T(8,128)(2,1)S(1)}, u32[]{:S(2)}, u32[]{:S(2)}) %collective-permute-start.1) | collective-permute-done | bytes 266272 | tf_op jit(solution)/shard_map/ppermute | solution.py:395
  23.3 0.1 add.10
  23.4 1.5 %collective-permute-start.2 = (bf16[1040,128]{1,0:T(8,128)(2,1)S(1)}, bf16[1040,128]{1,0:T(8,128)(2,1)S(1)}, u32[]{:S(2)}, u32[]{:S(2)}) collective-permute-start(bf16[1040,128]{1,0:T(8,128)(2,1)S(1)} %add.10), channel_id=1, source_target_pairs={{1,3},{9,11},{5,7},{13,15},{0,4},{2,6},{8,12},{10,14},{17,19},{25,... | collective-permute-start | bytes 798728 | tf_op jit(solution)/shard_map/ppermute | solution.py:395
  24.9 4.6 %first2.1 = (f32[512,512]{1,0:T(8,128)S(1)}, f32[2,512,512]{2,1,0:T(8,128)}) custom-call(f32[512,512]{1,0:T(8,128)S(1)} %get-tuple-element.14.refs_0_, f32[2,512,512]{2,1,0:T(8,128)} %get-tuple-element.15.refs_1_), custom_call_target="tpu_custom_call", output_to_operand_aliasing={{0}: (0, {}), {1}: (1, {})} | custom-call | flops 4000000000 | bytes 1000000 | tf_op jit(solution)/shard_map/first2/pallas_call | solution.py:379
  29.5 0.0 collective-permute-done.2
  29.5 0.1 add.11.got
  29.6 0.1 collective-permute-start.3
  29.6 0.0 copy-start.1
  29.7 0.0 copy-start.3
  29.7 0.0 copy-start.4
  29.7 0.0 copy-start.5
  29.7 0.0 copy-start.7
  29.7 0.0 copy-start.10
  29.7 4.3 %first3.1 = (f32[512,512]{1,0:T(8,128)S(1)}, f32[2,512,512]{2,1,0:T(8,128)}) custom-call(f32[512,512]{1,0:T(8,128)S(1)} %get-tuple-element.16.refs_0_, f32[2,512,512]{2,1,0:T(8,128)} %get-tuple-element.17.refs_1_), custom_call_target="tpu_custom_call", output_to_operand_aliasing={{0}: (0, {}), {1}: (1, {})} | custom-call | flops 4000000000 | bytes 1000000 | tf_op jit(solution)/shard_map/first3/pallas_call | solution.py:379
  34.0 0.0 collective-permute-done.3.came
  34.0 0.0 copy-done.1
  34.0 0.0 copy-done.3
  34.0 0.0 copy-done.4
  34.0 0.0 copy-done.5
  34.0 0.0 copy-done.7
  34.1 0.0 copy-done.10
  34.1 26.5 %second.1 = (f32[2,512,512]{2,1,0:T(8,128)}, f32[8,1,512,256]{3,2,1,0:T(8,128)}) custom-call(s32[3,2,512]{2,1,0:T(2,128)S(1)} %bitcast.5, s32[2,8]{1,0:T(2,128)S(1)} %bitcast.7, s32[8,1,512]{2,1,0:T(1,128)S(1)} %copy-done.7, bf16[1040,128]{1,0:T(8,128)(2,1)S(1)} %add.11.got, ...), custom_call_target="tpu_custom_call", output_to_operand_aliasing={{0}: (10, {})} | custom-call | tf_op jit(solution)/shard_map/second/pallas_call | solution.py:399
Async XLA Ops:
  0.6 1.2 %copy-start = (bf16[8,1,512,128]{3,2,1,0:T(8,128)(2,1)S(1)}, bf16[8,1,512,128]{3,2,1,0:T(8,128)(2,1)}, u32[]{:S(2)}) copy-start(bf16[8,1,512,128]{3,2,1,0:T(8,128)(2,1)} %u_first.1) | copy-start | bytes 3145732
  1.9 1.2 %copy-start.2 = (bf16[8,1,512,128]{3,2,1,0:T(8,128)(2,1)S(1)}, bf16[8,1,512,128]{3,2,1,0:T(8,128)(2,1)}, u32[]{:S(2)}) copy-start(bf16[8,1,512,128]{3,2,1,0:T(8,128)(2,1)} %v_first.1) | copy-start | bytes 3145732
  3.1 0.7 %copy-start.6 = (s32[8,1,512]{2,1,0:T(1,128)S(1)}, s32[8,1,512]{2,1,0:T(1,128)}, u32[]{:S(2)}) copy-start(s32[8,1,512]{2,1,0:T(1,128)} %label_rows.1) | copy-start | bytes 49156
  3.8 0.7 %copy-start.9 = (s32[8,1,2]{0,2,1:T(2,128)S(1)}, s32[8,1,2]{0,2,1:T(2,128)}, u32[]{:S(2)}) copy-start(s32[8,1,2]{0,2,1:T(2,128)} %param.9) | copy-start | bytes 196
  4.5 5.5 %copy-start.8 = (s32[2,3,512]{2,0,1:T(2,128)S(1)}, s32[2,3,512]{2,0,1:T(2,128)}, u32[]{:S(2)}) copy-start(s32[2,3,512]{2,0,1:T(2,128)} %param.7) | copy-start | bytes 36868
  5.1 10.1 %collective-permute-start = (bf16[1040,128]{1,0:T(8,128)(2,1)S(1)}, bf16[1040,128]{1,0:T(8,128)(2,1)S(1)}, u32[]{:S(2)}, u32[]{:S(2)}) collective-permute-start(bf16[1040,128]{1,0:T(8,128)(2,1)S(1)} %pack.1), channel_id=1, source_target_pairs={{1,9},{0,2},{17,25},{16,18}} | collective-permute-start | bytes 798728 | tf_op jit(solution)/shard_map/ppermute | solution.py:395
  15.3 8.0 %collective-permute-start.1 = (bf16[1040,128]{1,0:T(8,128)(2,1)S(1)}, bf16[1040,128]{1,0:T(8,128)(2,1)S(1)}, u32[]{:S(2)}, u32[]{:S(2)}) collective-permute-start(bf16[1040,128]{1,0:T(8,128)(2,1)S(1)} %add.9), channel_id=1, source_target_pairs={{1,5},{9,13},{0,8},{2,10},{17,21},{25,29},{16,24},{18,26}} | collective-permute-start | bytes 798728 | tf_op jit(solution)/shard_map/ppermute | solution.py:395
  23.4 6.1 %collective-permute-start.2 = (bf16[1040,128]{1,0:T(8,128)(2,1)S(1)}, bf16[1040,128]{1,0:T(8,128)(2,1)S(1)}, u32[]{:S(2)}, u32[]{:S(2)}) collective-permute-start(bf16[1040,128]{1,0:T(8,128)(2,1)S(1)} %add.10), channel_id=1, source_target_pairs={{1,3},{9,11},{5,7},{13,15},{0,4},{2,6},{8,12},{10,14},{17,19},{25,... | collective-permute-start | bytes 798728 | tf_op jit(solution)/shard_map/ppermute | solution.py:395
  29.6 4.4 %collective-permute-start.3 = (bf16[1040,128]{1,0:T(8,128)(2,1)S(1)}, bf16[1040,128]{1,0:T(8,128)(2,1)S(1)}, u32[]{:S(2)}, u32[]{:S(2)}) collective-permute-start(bf16[1040,128]{1,0:T(8,128)(2,1)S(1)} %add.11.got), channel_id=1, source_target_pairs={{0,1},{1,0},{2,3},{3,2},{4,5},{5,4},{6,7},{7,6},{8,9},{9,8},{10,11... | collective-permute-start | bytes 798728 | tf_op jit(solution)/shard_map/ppermute | solution.py:396
  29.6 4.4 %copy-start.1 = (bf16[8,1,512,128]{3,2,1,0:T(8,128)(2,1)S(1)}, bf16[8,1,512,128]{3,2,1,0:T(8,128)(2,1)}, u32[]{:S(2)}) copy-start(bf16[8,1,512,128]{3,2,1,0:T(8,128)(2,1)} %u_first.1) | copy-start | bytes 3145732
  29.7 4.4 %copy-start.3 = (bf16[8,1,512,128]{3,2,1,0:T(8,128)(2,1)S(1)}, bf16[8,1,512,128]{3,2,1,0:T(8,128)(2,1)}, u32[]{:S(2)}) copy-start(bf16[8,1,512,128]{3,2,1,0:T(8,128)(2,1)} %v_first.1) | copy-start | bytes 3145732
  29.7 4.4 %copy-start.4 = (bf16[8,1,512,128]{3,2,1,0:T(8,128)(2,1)S(1)}, bf16[8,1,512,128]{3,2,1,0:T(8,128)(2,1)}, u32[]{:S(2)}) copy-start(bf16[8,1,512,128]{3,2,1,0:T(8,128)(2,1)} %u_second.1) | copy-start | bytes 3145732
  29.7 4.4 %copy-start.5 = (bf16[8,1,512,128]{3,2,1,0:T(8,128)(2,1)S(1)}, bf16[8,1,512,128]{3,2,1,0:T(8,128)(2,1)}, u32[]{:S(2)}) copy-start(bf16[8,1,512,128]{3,2,1,0:T(8,128)(2,1)} %v_second.1) | copy-start | bytes 3145732
  29.7 4.4 %copy-start.7 = (s32[8,1,512]{2,1,0:T(1,128)S(1)}, s32[8,1,512]{2,1,0:T(1,128)}, u32[]{:S(2)}) copy-start(s32[8,1,512]{2,1,0:T(1,128)} %label_rows.1) | copy-start | bytes 49156
  29.7 4.4 %copy-start.10 = (s32[8,1,2]{0,2,1:T(2,128)S(1)}, s32[8,1,2]{0,2,1:T(2,128)}, u32[]{:S(2)}) copy-start(s32[8,1,2]{0,2,1:T(2,128)} %param.9) | copy-start | bytes 196

commit v3 on v2

--- a/solution.py
+++ b/solution.py
@@ -41,6 +41,21 @@
 
 def split_right(left, right, dims=NN, number=3):
     return sum(mul(left, piece, dims) for piece in reversed(parts_of(right, number)))
+
+
+def lower_left(product, lower, right):
+    size = lower.shape[0]
+    half = size // 2
+    return jnp.concatenate(
+        [product(lower[:half, :half], right[:half]), product(lower[half:, :], right)], axis=0
+    )
+
+
+def lower_right(left, lower):
+    half = lower.shape[0] // 2
+    return jnp.concatenate(
+        [mul(left, lower[:, :half], TN, high), mul(left[half:], lower[half:, half:], TN, high)], axis=1
+    )
 
 
 def row_of(value, index):
@@ -197,7 +212,7 @@
     return jnp.where(row == label_row, 1.0, 0.0).astype(f32)
 
 
-def pack_kernel(ranks, labels, u, v, packed):
+def pack(ranks, labels, u, v, packed):
     size, breadth = u.shape
     position = lax.axis_index("row")
     lane = lax.broadcasted_iota(jnp.int32, (size, breadth), 1)
@@ -215,13 +230,39 @@
     packed[2 * size :, :] = jnp.where(source == position, label, 0.0).astype(bf16)
 
 
-def first_kernel(k, *refs):
-    if k == 0:
-        coords, matrix, diagonal, strip, corner, panel, sem = refs
-        matrix[...] = kernel_tile(coords[:, 0, :])
-    else:
-        old, _, matrix, diagonal, strip, corner, panel, sem = refs
-        matrix[...] = old[...]
+def first_kernel(
+    coords, ranks, labels, u_first, v_first,
+    matrix, diagonal, packed,
+    strip, corner, panel, points, rank_rows, label_row, u_one, v_one, sem, sems,
+):
+    loads = [
+        pltpu.make_async_copy(source, target, sems.at[i])
+        for i, (source, target) in enumerate(
+            (
+                (coords, points),
+                (u_first.at[0, 0], u_one),
+                (v_first.at[0, 0], v_one),
+                (labels.at[0], label_row),
+                (ranks, rank_rows),
+            )
+        )
+    ]
+    for load in loads:
+        load.start()
+    loads[0].wait()
+    matrix[...] = kernel_tile(points[:, 0, :])
+    for load in loads[1:]:
+        load.wait()
+    pack(rank_rows, label_row, u_one, v_one, packed)
+    first_step(0, matrix, diagonal, strip, corner, panel, sem)
+
+
+def next_kernel(k, old, _, matrix, diagonal, strip, corner, panel, sem):
+    matrix[...] = old[...]
+    first_step(k, matrix, diagonal, strip, corner, panel, sem)
+
+
+def first_step(k, matrix, diagonal, strip, corner, panel, sem):
     factor_step(matrix, strip, corner, panel, k)
     copy = pltpu.make_async_copy(strip, diagonal.at[0, :, pl.ds(LANES * k, LANES)], sem)
     copy.start()
@@ -229,21 +270,13 @@
 
 
 def second_kernel(
-    coords, ranks, label_rows, got, came, inverse, u_first, v_first, u_second, v_second, _,
+    coords, ranks, label_rows, got, came, inverse, u0, v0, u1, v1, _,
     diagonal, out,
     matrix, strip, corner, panel, y_first, y_second, z_first, z_second, result,
-    u0, v0, u1, v1, in_sems, out_sems, strip_sems,
+    out_sems, strip_sems,
 ):
     size = inverse.shape[0]
     cycles = result.shape[0]
-    loads = [
-        pltpu.make_async_copy(source.at[:, 0], target, in_sems.at[i])
-        for i, (source, target) in enumerate(
-            ((u_first, u0), (v_first, v0), (u_second, u1), (v_second, v1))
-        )
-    ]
-    for load in loads:
-        load.start()
     shared = (got[...].astype(f32) + came[...].astype(f32))
     u_one = shared[0:size, :].astype(bf16)
     v_one = shared[size : 2 * size, :].astype(bf16)
@@ -258,12 +291,12 @@
     first_b = onehot_rows(label_row(0)).astype(bf16)
     y0 = split_left(inverse[...], first_b, NT)
     y_first[...] = y0
-    w_one = split_left(inverse[...], v_one)
+    w_one = lower_left(split_left, inverse[...], v_one)
     gram = mul(w_one, w_one, TN, highest)
     left = split_right(u_one, gram)
     matrix[...] = kernel_tile(coords[:, 1, :]) - split_left(left, u_one, NT)
     target = onehot_rows(label_row(1)).T - split_right(u_one, mul(w_one, y0, TN, highest))
-    z0 = mul(y0, inverse[...], TN, high)
+    z0 = lower_right(y0, inverse[...])
     p_one = mul(inverse[...], w_one, TN, high)
     strips = []
     for k in range(size // LANES):
@@ -273,17 +306,15 @@
         )
         copy.start()
         strips.append(copy)
-    y1 = mul(matrix[...], target, NN, high)
+    y1 = lower_left(functools.partial(mul, precision=high), matrix[...], target)
     y_second[...] = y1
-    z1 = mul(y1, matrix[...], TN, high)
+    z1 = lower_right(y1, matrix[...])
     q_one = split_left(z1, u_one, NN, 2)
     zc = z0 - mul(q_one, p_one, NT, high)
     for which, ref in ((zc, z_first), (z1, z_second)):
         big, small = parts_of(which, 2)
         ref[0:NRHS, :] = big
         ref[NRHS:, :] = small
-    for load in loads:
-        load.wait()
     columns = label_rows[:, 0, :].astype(f32).T
     lane = lax.broadcasted_iota(jnp.int32, (size, LANES), 1).astype(f32)
     keep = lax.broadcasted_iota(jnp.int32, (NRHS, LANES), 1)
@@ -293,7 +324,7 @@
         tiles = range(at, min(at + 2, cycles))
 
         def weights(v, z, which):
-            both = mul(z[...], jnp.concatenate([v[t] for t in tiles], axis=1))
+            both = mul(z[...], jnp.concatenate([v[t, 0] for t in tiles], axis=1))
             value = both[:NRHS] + both[NRHS:]
             return [
                 jnp.where(keep < ranks[which, t], value[:, LANES * i : LANES * (i + 1)], 0.0)
@@ -303,7 +334,7 @@
         h_first, h_second = weights(v0, z_first, 0), weights(v1, z_second, 1)
         for i, t in enumerate(tiles):
             both = jnp.concatenate([h_first[i], h_second[i]], axis=1)
-            total = split_right(jnp.concatenate([u0[t], u1[t]], axis=1), both, NT, 2)
+            total = split_right(jnp.concatenate([u0[t, 0], u1[t, 0]], axis=1), both, NT, 2)
             column = jnp.broadcast_to(columns[:, t : t + 1], (size, LANES))
             hot = jnp.concatenate(
                 [jnp.where(column == lane + float(LANES * j), 1.0, 0.0) for j in range(NRHS // LANES)],
@@ -355,51 +386,62 @@
 
     packed_size = 2 * size + 16
 
-    def one(width):
-        return pl.BlockSpec((None, None, size, width), lambda i: (0, 0, 0, 0))
-
-    packed = pl.pallas_call(
-        pack_kernel,
-        out_shape=jax.ShapeDtypeStruct((packed_size, breadth), bf16),
-        grid=(1,),
-        in_specs=[scalars, pl.BlockSpec((None, 1, size), lambda i: (0, 0, 0)), one(breadth), one(breadth)],
-        out_specs=pl.BlockSpec((packed_size, breadth), lambda i: (0, 0)),
-        compiler_params=pltpu.CompilerParams(vmem_limit_bytes=8 << 20),
-        name="pack",
-    )(rank_rows, labels, u_first, v_first)
-
     square = jax.ShapeDtypeStruct((size, size), f32)
     stack = jax.ShapeDtypeStruct((2, size, size), f32)
     room = [
         pltpu.VMEM((LANES, LANES), f32),
         pltpu.VMEM((LANES, size), f32),
     ]
-    state = (points,)
-    for k in range(blocks):
-        state = pl.pallas_call(
-            functools.partial(first_kernel, k),
-            out_shape=[square, stack],
-            in_specs=[whole] if k == 0 else [whole, anywhere],
-            out_specs=[whole, anywhere],
-            input_output_aliases={} if k == 0 else {0: 0, 1: 1},
-            scratch_shapes=[pltpu.VMEM((size, LANES), f32)] + room + [pltpu.SemaphoreType.DMA],
-            compiler_params=pltpu.CompilerParams(vmem_limit_bytes=12 << 20),
-            cost_estimate=pl.CostEstimate(flops=4 * 10**9, bytes_accessed=10**6, transcendentals=0),
-            name=f"first{k}",
-        )(*state)
-    inverse, diagonal = state
-
+    params = pltpu.CompilerParams(vmem_limit_bytes=12 << 20)
+    estimate = pl.CostEstimate(flops=4 * 10**9, bytes_accessed=10**6, transcendentals=0)
+    strip = [pltpu.VMEM((size, LANES), f32)]
+    inverse, diagonal, packed = pl.pallas_call(
+        first_kernel,
+        out_shape=[square, stack, jax.ShapeDtypeStruct((packed_size, breadth), bf16)],
+        in_specs=[pl.BlockSpec(memory_space=pltpu.HBM)] * 5,
+        out_specs=[whole, anywhere, whole],
+        scratch_shapes=strip
+        + room
+        + [
+            pltpu.VMEM(points.shape, jnp.int32),
+            pltpu.SMEM(rank_rows.shape, jnp.int32),
+            pltpu.VMEM((1, size), jnp.int32),
+            pltpu.VMEM((size, breadth), bf16),
+            pltpu.VMEM((size, breadth), bf16),
+            pltpu.SemaphoreType.DMA,
+            pltpu.SemaphoreType.DMA((5,)),
+        ],
+        compiler_params=params,
+        cost_estimate=estimate,
+        name="first0",
+    )(*(pltpu.with_memory_space_constraint(x, pltpu.HBM) for x in (points, rank_rows, labels, u_first, v_first)))
     got = packed
     pairs = hops(row_size)
-    for pair in pairs[:-1]:
+    for k in range(1, blocks):
+        late = lax.ppermute(got, "row", pairs[k - 1]) if k < len(pairs) else None
+        inverse, diagonal = pl.pallas_call(
+            functools.partial(next_kernel, k),
+            out_shape=[square, stack],
+            in_specs=[whole, anywhere],
+            out_specs=[whole, anywhere],
+            input_output_aliases={0: 0, 1: 1},
+            scratch_shapes=strip + room + [pltpu.SemaphoreType.DMA],
+            compiler_params=params,
+            cost_estimate=estimate,
+            name=f"first{k}",
+        )(inverse, diagonal)
+        if late is not None:
+            late, inverse = lax.optimization_barrier((late, inverse))
+            got = got + late
+
+    for pair in pairs[blocks - 1 : -1]:
         got = got + lax.ppermute(got, "row", pair)
     came = lax.ppermute(got, "row", pairs[-1])
 
-    slab = pltpu.VMEM((cycles, size, breadth), bf16)
     diagonal, eliminated = pl.pallas_call(
         second_kernel,
         out_shape=[stack, jax.ShapeDtypeStruct((cycles, 1, size, NRHS), f32)],
-        in_specs=[whole, scalars, whole, whole, whole, whole] + [anywhere] * 5,
+        in_specs=[whole, scalars] + [whole] * 8 + [anywhere],
         out_specs=[anywhere, anywhere],
         scratch_shapes=[
             pltpu.VMEM((size, size), f32),
@@ -410,8 +452,6 @@
             pltpu.VMEM((2 * NRHS, size), bf16),
             pltpu.VMEM((2 * NRHS, size), bf16),
             pltpu.VMEM((cycles, size, NRHS), f32),
-            slab, slab, slab, slab,
-            pltpu.SemaphoreType.DMA((4,)),
             pltpu.SemaphoreType.DMA((cycles,)),
             pltpu.SemaphoreType.DMA((blocks,)),
         ],

time: 61.1 us -> 57.4 us (0.939)
  local copies, waits for them, and re-layouts: 3.88 us -> 0.04 us
  waiting for transfers between devices: 1.38 us -> 3.18 us
  Pallas kernels: 46.1 us -> 44.5 us
    unnamed x22 -> x14, local copies, waits for them, and re-layouts: 3.88 us -> 0.04 us
    pallas_call x1, Pallas kernels: 26.5 us -> 24.6 us  [local(): pl.pallas_call(second_kernel, out_shape=[stack, jax.ShapeDtypeStruct((cyc...]
    ppermute x1, waiting for transfers between devices: 0.01 us -> 1.53 us  [local(): came = lax.ppermute(got, 'row', pairs[-1])]
    pallas_call x5 -> x4, Pallas kernels: 19.5 us -> 19.8 us  [the longest x3 13.7 us: local(): pl.pallas_call(functools.partial(next_kernel, k), out_shape=[square, stac...]
  transfers between devices with their start and end apart: 4 -> 4, of which waited for: 1 -> 2; matrix products, arithmetic and copies ran while one was open for 0% -> 0% of each run, Pallas kernels for 31% -> 24%
where the time goes in v3:
time: 57.4 us; the launch traced here: 57.1 us
  Pallas kernels  44.5 us (78%)
  starting transfers between devices  8.2 us (14%)
  waiting for transfers between devices  3.18 us (6%)
  between operations  1 us (2%)
    pallas_call x1, Pallas kernels, local(): pl.pallas_call(second_kernel, out_shape=[stack, jax.ShapeDtypeStruct((cyc...  24.6 us
    pallas_call x3, Pallas kernels, local(): pl.pallas_call(functools.partial(next_kernel, k), out_shape=[square, stac...  13.7 us
    ppermute x3, starting transfers between devices, local(): late = lax.ppermute(got, 'row', pairs[k - 1]) if k < len(pairs) else None  8.13 us
    pallas_call x1, Pallas kernels, local(): pl.pallas_call(first_kernel, out_shape=[square, stack, jax.ShapeDtypeStru...  6.1 us
    ppermute x3, waiting for transfers between devices, local(): late = lax.ppermute(got, 'row', pairs[k - 1]) if k < len(pairs) else None  1.65 us
    ppermute x1, waiting for transfers between devices, local(): came = lax.ppermute(got, 'row', pairs[-1])  1.53 us
  transfers between devices with their start and end apart: 4, of which 2 were waited for; matrix products, arithmetic and copies ran while one was open for 0% of the time, Pallas kernels for 24%

profile of v3, /device:TPU:0, one launch (start us, length us, event | category | flops | bytes accessed | tf_op | source)
XLA Modules:
  0.0 57.1 jit_solution(10860722836376200839)
XLA Ops:
  0.6 6.1 %first0.1 = (f32[512,512]{1,0:T(8,128)S(1)}, f32[2,512,512]{2,1,0:T(8,128)}, bf16[1040,128]{1,0:T(8,128)(2,1)S(1)}) custom-call(s32[3,2,512]{2,1,0:T(2,128)} %bitcast.4, s32[2,8]{1,0:T(2,128)} %bitcast.6, s32[8,1,512]{2,1,0:T(1,128)} %label_rows.1, bf16[8,1,512,128]{3,2,1,0:T(8,128)(2,1)} %u0.1, bf16[8,1,512,128]{3,2,1,0:T(8,128)(2,1)} %v0.1), custom_call_target="tpu_custom_call" | custom-call | flops 4000000000 | bytes 1000000 | tf_op jit(solution)/shard_map/first0/pallas_call | solution.py:398
  6.7 4.9 %collective-permute-start = (bf16[1040,128]{1,0:T(8,128)(2,1)S(1)}, bf16[1040,128]{1,0:T(8,128)(2,1)S(1)}, u32[]{:S(2)}, u32[]{:S(2)}) collective-permute-start(bf16[1040,128]{1,0:T(8,128)(2,1)S(1)} %get-tuple-element.19), channel_id=1, source_target_pairs={{1,9},{0,2},{17,25},{16,18}} | collective-permute-start | bytes 798728 | tf_op jit(solution)/shard_map/ppermute | solution.py:421
  11.6 4.9 %first1.1 = (f32[512,512]{1,0:T(8,128)S(1)}, f32[2,512,512]{2,1,0:T(8,128)}) custom-call(f32[512,512]{1,0:T(8,128)S(1)} %get-tuple-element.20.old, f32[2,512,512]{2,1,0:T(8,128)} %get-tuple-element.21._), custom_call_target="tpu_custom_call", output_to_operand_aliasing={{0}: (0, {}), {1}: (1, {})} | custom-call | flops 4000000000 | bytes 1000000 | tf_op jit(solution)/shard_map/first1/pallas_call | solution.py:422
  16.5 0.0 collective-permute-done
  16.5 0.1 add.9
  16.6 1.8 %collective-permute-start.1 = (bf16[1040,128]{1,0:T(8,128)(2,1)S(1)}, bf16[1040,128]{1,0:T(8,128)(2,1)S(1)}, u32[]{:S(2)}, u32[]{:S(2)}) collective-permute-start(bf16[1040,128]{1,0:T(8,128)(2,1)S(1)} %add.9), channel_id=1, source_target_pairs={{1,5},{9,13},{0,8},{2,10},{17,21},{25,29},{16,24},{18,26}} | collective-permute-start | bytes 798728 | tf_op jit(solution)/shard_map/ppermute | solution.py:421
  18.4 4.6 %first2.1 = (f32[512,512]{1,0:T(8,128)S(1)}, f32[2,512,512]{2,1,0:T(8,128)}) custom-call(f32[512,512]{1,0:T(8,128)S(1)} %get-tuple-element.24.old, f32[2,512,512]{2,1,0:T(8,128)} %get-tuple-element.25._), custom_call_target="tpu_custom_call", output_to_operand_aliasing={{0}: (0, {}), {1}: (1, {})} | custom-call | flops 4000000000 | bytes 1000000 | tf_op jit(solution)/shard_map/first2/pallas_call | solution.py:422
  23.0 1.6 %collective-permute-done.1 = bf16[1040,128]{1,0:T(8,128)(2,1)S(1)} collective-permute-done((bf16[1040,128]{1,0:T(8,128)(2,1)S(1)}, bf16[1040,128]{1,0:T(8,128)(2,1)S(1)}, u32[]{:S(2)}, u32[]{:S(2)}) %collective-permute-start.1) | collective-permute-done | bytes 266272 | tf_op jit(solution)/shard_map/ppermute | solution.py:421
  24.6 0.1 add.10
  24.7 1.5 %collective-permute-start.2 = (bf16[1040,128]{1,0:T(8,128)(2,1)S(1)}, bf16[1040,128]{1,0:T(8,128)(2,1)S(1)}, u32[]{:S(2)}, u32[]{:S(2)}) collective-permute-start(bf16[1040,128]{1,0:T(8,128)(2,1)S(1)} %add.10), channel_id=1, source_target_pairs={{1,3},{9,11},{5,7},{13,15},{0,4},{2,6},{8,12},{10,14},{17,19},{25,... | collective-permute-start | bytes 798728 | tf_op jit(solution)/shard_map/ppermute | solution.py:421
  26.2 0.0 copy-start
  26.2 0.0 copy-start.1
  26.2 0.0 copy-start.2
  26.2 0.0 copy-start.3
  26.2 0.0 copy-start.4
  26.2 0.0 copy-start.5
  26.2 0.0 copy-start.6
  26.3 4.3 %first3.1 = (f32[512,512]{1,0:T(8,128)S(1)}, f32[2,512,512]{2,1,0:T(8,128)}) custom-call(f32[512,512]{1,0:T(8,128)S(1)} %get-tuple-element.28.old, f32[2,512,512]{2,1,0:T(8,128)} %get-tuple-element.29._), custom_call_target="tpu_custom_call", output_to_operand_aliasing={{0}: (0, {}), {1}: (1, {})} | custom-call | flops 4000000000 | bytes 1000000 | tf_op jit(solution)/shard_map/first3/pallas_call | solution.py:422
  30.5 0.0 collective-permute-done.2
  30.6 0.1 add.11.got
  30.6 0.1 collective-permute-start.3
  30.7 1.5 %collective-permute-done.3.came = bf16[1040,128]{1,0:T(8,128)(2,1)S(1)} collective-permute-done((bf16[1040,128]{1,0:T(8,128)(2,1)S(1)}, bf16[1040,128]{1,0:T(8,128)(2,1)S(1)}, u32[]{:S(2)}, u32[]{:S(2)}) %collective-permute-start.3) | collective-permute-done | bytes 266272 | tf_op jit(solution)/shard_map/ppermute | solution.py:439
  32.2 0.0 copy-done
  32.2 0.0 copy-done.1
  32.2 0.0 copy-done.2
  32.3 0.0 copy-done.3
  32.3 0.0 copy-done.4
  32.3 0.0 copy-done.5
  32.3 0.0 copy-done.6
  32.3 24.6 %second.1 = (f32[2,512,512]{2,1,0:T(8,128)}, f32[8,1,512,256]{3,2,1,0:T(8,128)}) custom-call(s32[3,2,512]{2,1,0:T(2,128)S(1)} %bitcast.5, s32[2,8]{1,0:T(2,128)S(1)} %bitcast.7, s32[8,1,512]{2,1,0:T(1,128)S(1)} %copy-done.4, bf16[1040,128]{1,0:T(8,128)(2,1)S(1)} %add.11.got, ...), custom_call_target="tpu_custom_call", output_to_operand_aliasing={{0}: (10, {})} | custom-call | tf_op jit(solution)/shard_map/second/pallas_call | solution.py:441
Async XLA Ops:
  6.7 9.8 %collective-permute-start = (bf16[1040,128]{1,0:T(8,128)(2,1)S(1)}, bf16[1040,128]{1,0:T(8,128)(2,1)S(1)}, u32[]{:S(2)}, u32[]{:S(2)}) collective-permute-start(bf16[1040,128]{1,0:T(8,128)(2,1)S(1)} %get-tuple-element.19), channel_id=1, source_target_pairs={{1,9},{0,2},{17,25},{16,18}} | collective-permute-start | bytes 798728 | tf_op jit(solution)/shard_map/ppermute | solution.py:421
  16.6 8.0 %collective-permute-start.1 = (bf16[1040,128]{1,0:T(8,128)(2,1)S(1)}, bf16[1040,128]{1,0:T(8,128)(2,1)S(1)}, u32[]{:S(2)}, u32[]{:S(2)}) collective-permute-start(bf16[1040,128]{1,0:T(8,128)(2,1)S(1)} %add.9), channel_id=1, source_target_pairs={{1,5},{9,13},{0,8},{2,10},{17,21},{25,29},{16,24},{18,26}} | collective-permute-start | bytes 798728 | tf_op jit(solution)/shard_map/ppermute | solution.py:421
  24.7 5.9 %collective-permute-start.2 = (bf16[1040,128]{1,0:T(8,128)(2,1)S(1)}, bf16[1040,128]{1,0:T(8,128)(2,1)S(1)}, u32[]{:S(2)}, u32[]{:S(2)}) collective-permute-start(bf16[1040,128]{1,0:T(8,128)(2,1)S(1)} %add.10), channel_id=1, source_target_pairs={{1,3},{9,11},{5,7},{13,15},{0,4},{2,6},{8,12},{10,14},{17,19},{25,... | collective-permute-start | bytes 798728 | tf_op jit(solution)/shard_map/ppermute | solution.py:421
  26.2 6.1 %copy-start = (bf16[8,1,512,128]{3,2,1,0:T(8,128)(2,1)S(1)}, bf16[8,1,512,128]{3,2,1,0:T(8,128)(2,1)}, u32[]{:S(2)}) copy-start(bf16[8,1,512,128]{3,2,1,0:T(8,128)(2,1)} %u0.1) | copy-start | bytes 3145732
  26.2 6.1 %copy-start.1 = (bf16[8,1,512,128]{3,2,1,0:T(8,128)(2,1)S(1)}, bf16[8,1,512,128]{3,2,1,0:T(8,128)(2,1)}, u32[]{:S(2)}) copy-start(bf16[8,1,512,128]{3,2,1,0:T(8,128)(2,1)} %v0.1) | copy-start | bytes 3145732
  26.2 6.1 %copy-start.2 = (bf16[8,1,512,128]{3,2,1,0:T(8,128)(2,1)S(1)}, bf16[8,1,512,128]{3,2,1,0:T(8,128)(2,1)}, u32[]{:S(2)}) copy-start(bf16[8,1,512,128]{3,2,1,0:T(8,128)(2,1)} %u1_.1) | copy-start | bytes 3145732
  26.2 6.0 %copy-start.3 = (bf16[8,1,512,128]{3,2,1,0:T(8,128)(2,1)S(1)}, bf16[8,1,512,128]{3,2,1,0:T(8,128)(2,1)}, u32[]{:S(2)}) copy-start(bf16[8,1,512,128]{3,2,1,0:T(8,128)(2,1)} %v1.1) | copy-start | bytes 3145732
  26.2 6.0 %copy-start.4 = (s32[8,1,512]{2,1,0:T(1,128)S(1)}, s32[8,1,512]{2,1,0:T(1,128)}, u32[]{:S(2)}) copy-start(s32[8,1,512]{2,1,0:T(1,128)} %label_rows.1) | copy-start | bytes 49156
  26.2 6.0 %copy-start.5 = (s32[2,3,512]{2,0,1:T(2,128)S(1)}, s32[2,3,512]{2,0,1:T(2,128)}, u32[]{:S(2)}) copy-start(s32[2,3,512]{2,0,1:T(2,128)} %param.7) | copy-start | bytes 36868
  26.2 6.0 %copy-start.6 = (s32[8,1,2]{0,2,1:T(2,128)S(1)}, s32[8,1,2]{0,2,1:T(2,128)}, u32[]{:S(2)}) copy-start(s32[8,1,2]{0,2,1:T(2,128)} %param.9) | copy-start | bytes 196
  30.6 1.6 %collective-permute-start.3 = (bf16[1040,128]{1,0:T(8,128)(2,1)S(1)}, bf16[1040,128]{1,0:T(8,128)(2,1)S(1)}, u32[]{:S(2)}, u32[]{:S(2)}) collective-permute-start(bf16[1040,128]{1,0:T(8,128)(2,1)S(1)} %add.11.got), channel_id=1, source_target_pairs={{0,1},{1,0},{2,3},{3,2},{4,5},{5,4},{6,7},{7,6},{8,9},{9,8},{10,11... | collective-permute-start | bytes 798728 | tf_op jit(solution)/shard_map/ppermute | solution.py:439

commit v4 on v3

--- a/solution.py
+++ b/solution.py
@@ -11,7 +11,6 @@
 NRHS = 256
 LANES = 128
 SUB = 8
-HALF = 64
 f32 = jnp.float32
 bf16 = jnp.bfloat16
 highest = lax.Precision.HIGHEST
@@ -66,102 +65,92 @@
     return jnp.broadcast_to(value[:, index : index + 1], value.shape)
 
 
-def factor_half(rows, base, put):
+def tree_sum(terms):
+    while len(terms) > 1:
+        terms = [terms[k] + terms[k + 1] for k in range(0, len(terms), 2)]
+    return terms[0]
+
+
+def factor_block(rows, put):
     number = len(rows)
     lane = lax.broadcasted_iota(jnp.int32, (SUB, LANES), 1)
     sub = lax.broadcasted_iota(jnp.int32, (SUB, LANES), 0)
     pair = range(2)
+    zero = jnp.zeros((SUB, LANES), f32)
     for step in range(0, number, 2):
-        low = SUB * (base + step)
+        low = SUB * step
         here = (lane >= low) & (lane < low + 2 * SUB)
-        columns = [[column_of(rows[i], low + c) for c in range(2 * SUB)] for i in range(step, number)]
+        far = step + 4
+        columns = [
+            [column_of(rows[i], low + c) for c in range(2 * SUB)]
+            for i in range(step, min(number, far))
+        ]
         pivot = [list(columns[0]), list(columns[1])]
         plain = [rows[step], rows[step + 1]]
         work = [
             jnp.where(here, jnp.where(lane - low == sub + SUB * g, 1.0, 0.0).astype(f32), plain[g])
             for g in pair
         ]
-        upper = [jnp.zeros((SUB, LANES), f32)] * 2
-        inverse = [jnp.zeros((SUB, LANES), f32)] * 2
+        upper, inverse, roots = [zero] * 2, [zero] * 2, [zero] * 2
         for first in range(0, 2 * SUB, 2):
             second = first + 1
             home, top, bottom = first // SUB, first % SUB, first % SUB + 1
             left, right = pivot[home][first], pivot[home][second]
             a, b, c = row_of(left, top), row_of(left, bottom), row_of(right, bottom)
-            scale = 1.0 / (a * c - b * b)
+            det = a * c - b * b
+            scale = 1.0 / det
             is_top, is_bottom = sub == top, sub == bottom
-            both = is_top | is_bottom
-            m_top, m_bottom = [], []
-            for g in pair:
+            m_top, m_bottom = {}, {}
+            for g in pair[home:]:
                 p = pivot[g][first] * c - pivot[g][second] * b
                 q = pivot[g][second] * a - pivot[g][first] * b
                 if g == home:
-                    p = jnp.where(is_top, -c, jnp.where(is_bottom, b, p))
-                    q = jnp.where(is_top, b, jnp.where(is_bottom, -a, q))
-                m_top.append(p * scale)
-                m_bottom.append(q * scale)
+                    p = jnp.where(is_top, det - c, jnp.where(is_bottom, b, p))
+                    q = jnp.where(is_top, b, jnp.where(is_bottom, det - a, q))
+                m_top[g], m_bottom[g] = p * scale, q * scale
 
             def eliminate(g, value, above, below):
-                kept = jnp.where(both, 0.0, value) if g == home else value
-                return kept - m_top[g] * above - m_bottom[g] * below
+                return value - m_top[g] * above - m_bottom[g] * below
 
             w_top, w_bottom = row_of(work[home], top), row_of(work[home], bottom)
             p_top, p_bottom = row_of(plain[home], top), row_of(plain[home], bottom)
-            root = lax.rsqrt(a)
-            factor = b * root
-            last = lax.rsqrt(c - factor * factor)
+            ratio = b * (1.0 / a)
+            after = sub >= top
             upper[home] = jnp.where(
-                is_top,
-                p_top * root,
-                jnp.where(is_bottom, (p_bottom - factor * (p_top * root)) * last, upper[home]),
+                after, jnp.where(is_top, p_top, p_bottom - ratio * p_top), upper[home]
             )
             inverse[home] = jnp.where(
-                is_top,
-                w_top * root,
-                jnp.where(is_bottom, (w_bottom - factor * (w_top * root)) * last, inverse[home]),
+                after, jnp.where(is_top, w_top, w_bottom - ratio * w_top), inverse[home]
+            )
+            roots[home] = jnp.where(
+                after, jnp.where(is_top, lax.rsqrt(a), lax.rsqrt(c - b * ratio)), roots[home]
             )
             for other in range(second + 1, 2 * SUB):
                 above, below = row_of(pivot[home][other], top), row_of(pivot[home][other], bottom)
-                for g in pair:
+                for g in pair[home:]:
                     pivot[g][other] = eliminate(g, pivot[g][other], above, below)
-            work = [eliminate(g, work[g], w_top, w_bottom) for g in pair]
-            plain = [
-                eliminate(g, plain[g], p_top, p_bottom) if g >= home else plain[g] for g in pair
-            ]
+            for g in pair[home:]:
+                work[g] = eliminate(g, work[g], w_top, w_bottom)
+                plain[g] = eliminate(g, plain[g], p_top, p_bottom)
         for g in pair:
             put(
                 step + g,
-                jnp.where(lane - low >= sub + SUB * g, upper[g], 0.0),
-                jnp.where(lane - low <= sub + SUB * g, inverse[g], 0.0),
+                jnp.where(lane - low >= sub + SUB * g, upper[g] * roots[g], 0.0),
+                jnp.where(lane - low <= sub + SUB * g, inverse[g] * roots[g], 0.0),
             )
         if step + 2 < number:
-            solved = [row_of(work[c // SUB], c % SUB) for c in range(2 * SUB)]
+            solved = [row_of(work[1], c) for c in range(SUB)]
+            work[0] = work[0] - tree_sum([pivot[0][SUB + c] * solved[c] for c in range(SUB)])
+            solved = [row_of(work[0], c) for c in range(SUB)] + solved
+            if far < number:
+                spread = jnp.concatenate([zero] * step + work + [zero] * (number - 2 - step), axis=0)
+                change = mul(jnp.concatenate(rows[far:], axis=0), spread, NN, highest)
             for i in range(step + 2, number):
-                terms = [columns[i - step][c] * solved[c] for c in range(2 * SUB)]
-                while len(terms) > 1:
-                    terms = [terms[k] + terms[k + 1] for k in range(0, len(terms), 2)]
-                rows[i] = jnp.where(here, 0.0, rows[i]) - terms[0]
-
-
-def factor_block(rows, put):
-    lane = lax.broadcasted_iota(jnp.int32, (SUB, LANES), 1)
-    group = HALF // SUB
-    for half in range(LANES // HALF):
-        done = [None] * group
-
-        def put_half(step, upper_rows, inverse_rows):
-            put(group * half + step, upper_rows, inverse_rows)
-            done[step] = jnp.where(lane < HALF * (half + 1), inverse_rows, upper_rows)
-
-        chosen = rows[group * half : group * (half + 1)]
-        factor_half(chosen, group * half, put_half)
-        if half == 0:
-            panel = jnp.concatenate(done, axis=0)
-            change = mul(panel.T[HALF:], panel, NN, highest)
-            for i in range(group):
-                rows[group + i] = (
-                    jnp.where(lane >= HALF, rows[group + i], 0.0) - change[SUB * i : SUB * (i + 1)]
-                )
+                if i < far:
+                    update = tree_sum([columns[i - step][c] * solved[c] for c in range(2 * SUB)])
+                else:
+                    update = change[SUB * (i - far) : SUB * (i - far + 1)]
+                rows[i] = jnp.where(here, 0.0, rows[i]) - update
 
 
 def factor_step(matrix, strip, corner, panel, k):

time: 57.4 us -> 53.8 us (0.937)
  Pallas kernels: 44.5 us -> 39.7 us
  waiting for transfers between devices: 3.18 us -> 3.78 us
    pallas_call x1, Pallas kernels: 24.6 us -> 22.3 us  [local(): pl.pallas_call(second_kernel, out_shape=[stack, jax.ShapeDtypeStruct((cyc...]
    pallas_call x3, Pallas kernels: 13.7 us -> 11.9 us  [local(): pl.pallas_call(functools.partial(next_kernel, k), out_shape=[square, stac...]
    ppermute x3, waiting for transfers between devices: 1.65 us -> 2.26 us  [local(): late = lax.ppermute(got, 'row', pairs[k - 1]) if k < len(pairs) else None]
    pallas_call x1, Pallas kernels: 6.1 us -> 5.5 us  [local(): pl.pallas_call(first_kernel, out_shape=[square, stack, jax.ShapeDtypeStru...]
  transfers between devices with their start and end apart: 4 -> 4, of which waited for: 2 -> 2; matrix products, arithmetic and copies ran while one was open for 0% -> 0% of each run, Pallas kernels for 24% -> 22%
where the time goes in v4:
time: 53.8 us; the launch traced here: 53 us
  Pallas kernels  39.7 us (74%)
  starting transfers between devices  8.19 us (15%)
  waiting for transfers between devices  3.78 us (7%)
  between operations  1 us (2%)
    pallas_call x1, Pallas kernels, local(): pl.pallas_call(second_kernel, out_shape=[stack, jax.ShapeDtypeStruct((cyc...  22.3 us
    pallas_call x3, Pallas kernels, local(): pl.pallas_call(functools.partial(next_kernel, k), out_shape=[square, stac...  11.9 us
    ppermute x3, starting transfers between devices, local(): late = lax.ppermute(got, 'row', pairs[k - 1]) if k < len(pairs) else None  8.12 us
    pallas_call x1, Pallas kernels, local(): pl.pallas_call(first_kernel, out_shape=[square, stack, jax.ShapeDtypeStru...  5.5 us
    ppermute x3, waiting for transfers between devices, local(): late = lax.ppermute(got, 'row', pairs[k - 1]) if k < len(pairs) else None  2.26 us
    ppermute x1, waiting for transfers between devices, local(): came = lax.ppermute(got, 'row', pairs[-1])  1.53 us
  transfers between devices with their start and end apart: 4, of which 2 were waited for; matrix products, arithmetic and copies ran while one was open for 0% of the time, Pallas kernels for 22%

profile of v4, /device:TPU:0, one launch (start us, length us, event | category | flops | bytes accessed | tf_op | source)
XLA Modules:
  0.0 53.0 jit_solution(12291476706045748482)
XLA Ops:
  0.6 5.5 %first0.1 = (f32[512,512]{1,0:T(8,128)S(1)}, f32[2,512,512]{2,1,0:T(8,128)}, bf16[1040,128]{1,0:T(8,128)(2,1)S(1)}) custom-call(s32[3,2,512]{2,1,0:T(2,128)} %bitcast.4, s32[2,8]{1,0:T(2,128)} %bitcast.6, s32[8,1,512]{2,1,0:T(1,128)} %label_rows.1, bf16[8,1,512,128]{3,2,1,0:T(8,128)(2,1)} %u0.1, bf16[8,1,512,128]{3,2,1,0:T(8,128)(2,1)} %v0.1), custom_call_target="tpu_custom_call" | custom-call | flops 4000000000 | bytes 1000000 | tf_op jit(solution)/shard_map/first0/pallas_call | solution.py:387
  6.1 4.9 %collective-permute-start = (bf16[1040,128]{1,0:T(8,128)(2,1)S(1)}, bf16[1040,128]{1,0:T(8,128)(2,1)S(1)}, u32[]{:S(2)}, u32[]{:S(2)}) collective-permute-start(bf16[1040,128]{1,0:T(8,128)(2,1)S(1)} %get-tuple-element.19), channel_id=1, source_target_pairs={{1,9},{0,2},{17,25},{16,18}} | collective-permute-start | bytes 798728 | tf_op jit(solution)/shard_map/ppermute | solution.py:410
  11.0 4.3 %first1.1 = (f32[512,512]{1,0:T(8,128)S(1)}, f32[2,512,512]{2,1,0:T(8,128)}) custom-call(f32[512,512]{1,0:T(8,128)S(1)} %get-tuple-element.20.old, f32[2,512,512]{2,1,0:T(8,128)} %get-tuple-element.21._), custom_call_target="tpu_custom_call", output_to_operand_aliasing={{0}: (0, {}), {1}: (1, {})} | custom-call | flops 4000000000 | bytes 1000000 | tf_op jit(solution)/shard_map/first1/pallas_call | solution.py:411
  15.3 0.0 collective-permute-done
  15.3 0.1 add.9
  15.4 1.7 %collective-permute-start.1 = (bf16[1040,128]{1,0:T(8,128)(2,1)S(1)}, bf16[1040,128]{1,0:T(8,128)(2,1)S(1)}, u32[]{:S(2)}, u32[]{:S(2)}) collective-permute-start(bf16[1040,128]{1,0:T(8,128)(2,1)S(1)} %add.9), channel_id=1, source_target_pairs={{1,5},{9,13},{0,8},{2,10},{17,21},{25,29},{16,24},{18,26}} | collective-permute-start | bytes 798728 | tf_op jit(solution)/shard_map/ppermute | solution.py:410
  17.2 4.0 %first2.1 = (f32[512,512]{1,0:T(8,128)S(1)}, f32[2,512,512]{2,1,0:T(8,128)}) custom-call(f32[512,512]{1,0:T(8,128)S(1)} %get-tuple-element.24.old, f32[2,512,512]{2,1,0:T(8,128)} %get-tuple-element.25._), custom_call_target="tpu_custom_call", output_to_operand_aliasing={{0}: (0, {}), {1}: (1, {})} | custom-call | flops 4000000000 | bytes 1000000 | tf_op jit(solution)/shard_map/first2/pallas_call | solution.py:411
  21.2 2.3 %collective-permute-done.1 = bf16[1040,128]{1,0:T(8,128)(2,1)S(1)} collective-permute-done((bf16[1040,128]{1,0:T(8,128)(2,1)S(1)}, bf16[1040,128]{1,0:T(8,128)(2,1)S(1)}, u32[]{:S(2)}, u32[]{:S(2)}) %collective-permute-start.1) | collective-permute-done | bytes 266272 | tf_op jit(solution)/shard_map/ppermute | solution.py:410
  23.4 0.1 add.10
  23.5 1.5 %collective-permute-start.2 = (bf16[1040,128]{1,0:T(8,128)(2,1)S(1)}, bf16[1040,128]{1,0:T(8,128)(2,1)S(1)}, u32[]{:S(2)}, u32[]{:S(2)}) collective-permute-start(bf16[1040,128]{1,0:T(8,128)(2,1)S(1)} %add.10), channel_id=1, source_target_pairs={{1,3},{9,11},{5,7},{13,15},{0,4},{2,6},{8,12},{10,14},{17,19},{25,... | collective-permute-start | bytes 798728 | tf_op jit(solution)/shard_map/ppermute | solution.py:410
  25.0 0.0 copy-start
  25.0 0.0 copy-start.1
  25.0 0.0 copy-start.2
  25.0 0.0 copy-start.3
  25.1 0.0 copy-start.4
  25.1 0.0 copy-start.5
  25.1 0.0 copy-start.6
  25.1 3.6 %first3.1 = (f32[512,512]{1,0:T(8,128)S(1)}, f32[2,512,512]{2,1,0:T(8,128)}) custom-call(f32[512,512]{1,0:T(8,128)S(1)} %get-tuple-element.28.old, f32[2,512,512]{2,1,0:T(8,128)} %get-tuple-element.29._), custom_call_target="tpu_custom_call", output_to_operand_aliasing={{0}: (0, {}), {1}: (1, {})} | custom-call | flops 4000000000 | bytes 1000000 | tf_op jit(solution)/shard_map/first3/pallas_call | solution.py:411
  28.7 0.0 collective-permute-done.2
  28.7 0.1 add.11.got
  28.8 0.1 collective-permute-start.3
  28.9 1.5 %collective-permute-done.3.came = bf16[1040,128]{1,0:T(8,128)(2,1)S(1)} collective-permute-done((bf16[1040,128]{1,0:T(8,128)(2,1)S(1)}, bf16[1040,128]{1,0:T(8,128)(2,1)S(1)}, u32[]{:S(2)}, u32[]{:S(2)}) %collective-permute-start.3) | collective-permute-done | bytes 266272 | tf_op jit(solution)/shard_map/ppermute | solution.py:428
  30.4 0.0 copy-done
  30.4 0.0 copy-done.1
  30.4 0.0 copy-done.2
  30.4 0.0 copy-done.3
  30.4 0.0 copy-done.4
  30.5 0.0 copy-done.5
  30.5 0.0 copy-done.6
  30.5 22.3 %second.1 = (f32[2,512,512]{2,1,0:T(8,128)}, f32[8,1,512,256]{3,2,1,0:T(8,128)}) custom-call(s32[3,2,512]{2,1,0:T(2,128)S(1)} %bitcast.5, s32[2,8]{1,0:T(2,128)S(1)} %bitcast.7, s32[8,1,512]{2,1,0:T(1,128)S(1)} %copy-done.4, bf16[1040,128]{1,0:T(8,128)(2,1)S(1)} %add.11.got, ...), custom_call_target="tpu_custom_call", output_to_operand_aliasing={{0}: (10, {})} | custom-call | tf_op jit(solution)/shard_map/second/pallas_call | solution.py:430
Async XLA Ops:
  6.1 9.2 %collective-permute-start = (bf16[1040,128]{1,0:T(8,128)(2,1)S(1)}, bf16[1040,128]{1,0:T(8,128)(2,1)S(1)}, u32[]{:S(2)}, u32[]{:S(2)}) collective-permute-start(bf16[1040,128]{1,0:T(8,128)(2,1)S(1)} %get-tuple-element.19), channel_id=1, source_target_pairs={{1,9},{0,2},{17,25},{16,18}} | collective-permute-start | bytes 798728 | tf_op jit(solution)/shard_map/ppermute | solution.py:410
  15.4 8.0 %collective-permute-start.1 = (bf16[1040,128]{1,0:T(8,128)(2,1)S(1)}, bf16[1040,128]{1,0:T(8,128)(2,1)S(1)}, u32[]{:S(2)}, u32[]{:S(2)}) collective-permute-start(bf16[1040,128]{1,0:T(8,128)(2,1)S(1)} %add.9), channel_id=1, source_target_pairs={{1,5},{9,13},{0,8},{2,10},{17,21},{25,29},{16,24},{18,26}} | collective-permute-start | bytes 798728 | tf_op jit(solution)/shard_map/ppermute | solution.py:410
  23.5 5.2 %collective-permute-start.2 = (bf16[1040,128]{1,0:T(8,128)(2,1)S(1)}, bf16[1040,128]{1,0:T(8,128)(2,1)S(1)}, u32[]{:S(2)}, u32[]{:S(2)}) collective-permute-start(bf16[1040,128]{1,0:T(8,128)(2,1)S(1)} %add.10), channel_id=1, source_target_pairs={{1,3},{9,11},{5,7},{13,15},{0,4},{2,6},{8,12},{10,14},{17,19},{25,... | collective-permute-start | bytes 798728 | tf_op jit(solution)/shard_map/ppermute | solution.py:410
  25.0 5.4 %copy-start = (bf16[8,1,512,128]{3,2,1,0:T(8,128)(2,1)S(1)}, bf16[8,1,512,128]{3,2,1,0:T(8,128)(2,1)}, u32[]{:S(2)}) copy-start(bf16[8,1,512,128]{3,2,1,0:T(8,128)(2,1)} %u0.1) | copy-start | bytes 3145732
  25.0 5.4 %copy-start.1 = (bf16[8,1,512,128]{3,2,1,0:T(8,128)(2,1)S(1)}, bf16[8,1,512,128]{3,2,1,0:T(8,128)(2,1)}, u32[]{:S(2)}) copy-start(bf16[8,1,512,128]{3,2,1,0:T(8,128)(2,1)} %v0.1) | copy-start | bytes 3145732
  25.0 5.4 %copy-start.2 = (bf16[8,1,512,128]{3,2,1,0:T(8,128)(2,1)S(1)}, bf16[8,1,512,128]{3,2,1,0:T(8,128)(2,1)}, u32[]{:S(2)}) copy-start(bf16[8,1,512,128]{3,2,1,0:T(8,128)(2,1)} %u1_.1) | copy-start | bytes 3145732
  25.0 5.4 %copy-start.3 = (bf16[8,1,512,128]{3,2,1,0:T(8,128)(2,1)S(1)}, bf16[8,1,512,128]{3,2,1,0:T(8,128)(2,1)}, u32[]{:S(2)}) copy-start(bf16[8,1,512,128]{3,2,1,0:T(8,128)(2,1)} %v1.1) | copy-start | bytes 3145732
  25.1 5.4 %copy-start.4 = (s32[8,1,512]{2,1,0:T(1,128)S(1)}, s32[8,1,512]{2,1,0:T(1,128)}, u32[]{:S(2)}) copy-start(s32[8,1,512]{2,1,0:T(1,128)} %label_rows.1) | copy-start | bytes 49156
  25.1 5.4 %copy-start.5 = (s32[2,3,512]{2,0,1:T(2,128)S(1)}, s32[2,3,512]{2,0,1:T(2,128)}, u32[]{:S(2)}) copy-start(s32[2,3,512]{2,0,1:T(2,128)} %param.7) | copy-start | bytes 36868
  25.1 5.4 %copy-start.6 = (s32[8,1,2]{0,2,1:T(2,128)S(1)}, s32[8,1,2]{0,2,1:T(2,128)}, u32[]{:S(2)}) copy-start(s32[8,1,2]{0,2,1:T(2,128)} %param.9) | copy-start | bytes 196
  28.8 1.6 %collective-permute-start.3 = (bf16[1040,128]{1,0:T(8,128)(2,1)S(1)}, bf16[1040,128]{1,0:T(8,128)(2,1)S(1)}, u32[]{:S(2)}, u32[]{:S(2)}) collective-permute-start(bf16[1040,128]{1,0:T(8,128)(2,1)S(1)} %add.11.got), channel_id=1, source_target_pairs={{0,1},{1,0},{2,3},{3,2},{4,5},{5,4},{6,7},{7,6},{8,9},{9,8},{10,11... | collective-permute-start | bytes 798728 | tf_op jit(solution)/shard_map/ppermute | solution.py:428

commit v5 on v4

--- a/solution.py
+++ b/solution.py
@@ -50,10 +50,18 @@
     )
 
 
-def lower_right(left, lower):
+def right_lower(left, lower):
     half = lower.shape[0] // 2
     return jnp.concatenate(
-        [mul(left, lower[:, :half], TN, high), mul(left[half:], lower[half:, half:], TN, high)], axis=1
+        [mul(left, lower[:, :half], NN, high), mul(left[:, half:], lower[half:, half:], NN, high)],
+        axis=1,
+    )
+
+
+def right_upper(product, left, lower):
+    half = lower.shape[0] // 2
+    return jnp.concatenate(
+        [product(left[:, :half], lower[:half, :half], NT), product(left, lower[half:, :], NT)], axis=1
     )
 
 
@@ -201,48 +209,56 @@
     return jnp.where(row == label_row, 1.0, 0.0).astype(f32)
 
 
-def pack(ranks, labels, u, v, packed):
-    size, breadth = u.shape
+def pack_kernel(ranks, labels, u_first, v_first, packed, rank_rows, label_row, u_one, v_one, sems):
+    size, breadth = u_one.shape
+    spread = size // breadth
     position = lax.axis_index("row")
-    lane = lax.broadcasted_iota(jnp.int32, (size, breadth), 1)
-    own = position == 1
-    packed[0:size, :] = jnp.where(own, u[...], 0).astype(bf16)
-    packed[size : 2 * size, :] = jnp.where(own & (lane < ranks[0, 0]), v[...], 0).astype(bf16)
-    spread = size // breadth
-    label = jnp.concatenate(
-        [labels[:, breadth * i : breadth * (i + 1)].astype(f32) for i in range(spread)] * 2
-        + [jnp.zeros((16 - 2 * spread, breadth), f32)],
-        axis=0,
-    )
-    row = lax.broadcasted_iota(jnp.int32, label.shape, 0)
-    source = jnp.where(row < spread, 0, 1)
-    packed[2 * size :, :] = jnp.where(source == position, label, 0.0).astype(bf16)
-
-
-def first_kernel(
-    coords, ranks, labels, u_first, v_first,
-    matrix, diagonal, packed,
-    strip, corner, panel, points, rank_rows, label_row, u_one, v_one, sem, sems,
-):
-    loads = [
-        pltpu.make_async_copy(source, target, sems.at[i])
-        for i, (source, target) in enumerate(
-            (
-                (coords, points),
-                (u_first.at[0, 0], u_one),
-                (v_first.at[0, 0], v_one),
-                (labels.at[0], label_row),
-                (ranks, rank_rows),
-            )
+    blank = jnp.zeros((size, breadth), bf16)
+
+    @pl.when(position > 1)
+    def _():
+        packed[0:size, :] = blank
+        packed[size : 2 * size, :] = blank
+        packed[2 * size :, :] = blank[:16]
+
+    @pl.when(position <= 1)
+    def _():
+        loads = [
+            pltpu.make_async_copy(source, target, sems.at[i])
+            for i, (source, target) in enumerate(
+                (
+                    (u_first.at[0, 0], u_one),
+                    (v_first.at[0, 0], v_one),
+                    (labels.at[0], label_row),
+                    (ranks, rank_rows),
+                )
+            )
+        ]
+        for load in loads:
+            load.start()
+        for load in loads:
+            load.wait()
+        lane = lax.broadcasted_iota(jnp.int32, (size, breadth), 1)
+        own = position == 1
+        packed[0:size, :] = jnp.where(own, u_one[...], 0).astype(bf16)
+        packed[size : 2 * size, :] = jnp.where(own & (lane < rank_rows[0, 0]), v_one[...], 0).astype(
+            bf16
         )
-    ]
-    for load in loads:
-        load.start()
-    loads[0].wait()
+        label = jnp.concatenate(
+            [label_row[:, breadth * i : breadth * (i + 1)].astype(f32) for i in range(spread)] * 2
+            + [jnp.zeros((16 - 2 * spread, breadth), f32)],
+            axis=0,
+        )
+        row = lax.broadcasted_iota(jnp.int32, label.shape, 0)
+        source = jnp.where(row < spread, 0, 1)
+        packed[2 * size :, :] = jnp.where(source == position, label, 0.0).astype(bf16)
+
+
+def first_kernel(coords, matrix, diagonal, strip, corner, panel, points, sem):
+    load = pltpu.make_async_copy(coords, points, sem)
+    load.start()
+    load.wait()
     matrix[...] = kernel_tile(points[:, 0, :])
-    for load in loads[1:]:
-        load.wait()
-    pack(rank_rows, label_row, u_one, v_one, packed)
     first_step(0, matrix, diagonal, strip, corner, panel, sem)
 
 
@@ -278,15 +294,16 @@
         )
 
     first_b = onehot_rows(label_row(0)).astype(bf16)
-    y0 = split_left(inverse[...], first_b, NT)
-    y_first[...] = y0
     w_one = lower_left(split_left, inverse[...], v_one)
-    gram = mul(w_one, w_one, TN, highest)
+    w_flat = w_one.T
+    gram = mul(w_flat, w_one, NN, highest)
     left = split_right(u_one, gram)
     matrix[...] = kernel_tile(coords[:, 1, :]) - split_left(left, u_one, NT)
-    target = onehot_rows(label_row(1)).T - split_right(u_one, mul(w_one, y0, TN, highest))
-    z0 = lower_right(y0, inverse[...])
-    p_one = mul(inverse[...], w_one, TN, high)
+    y0 = right_upper(split_right, first_b, inverse)
+    y_first[...] = y0
+    target = onehot_rows(label_row(1)) - split_left(mul(y0, w_one, NN, highest), u_one, NT)
+    z0 = right_lower(y0, inverse)
+    p_one = right_lower(w_flat, inverse)
     strips = []
     for k in range(size // LANES):
         factor_step(matrix, strip.at[k], corner, panel, k)
@@ -295,11 +312,11 @@
         )
         copy.start()
         strips.append(copy)
-    y1 = lower_left(functools.partial(mul, precision=high), matrix[...], target)
+    y1 = right_upper(functools.partial(mul, precision=high), target, matrix)
     y_second[...] = y1
-    z1 = lower_right(y1, matrix[...])
+    z1 = right_lower(y1, matrix)
     q_one = split_left(z1, u_one, NN, 2)
-    zc = z0 - mul(q_one, p_one, NT, high)
+    zc = z0 - mul(q_one, p_one, NN, high)
     for which, ref in ((zc, z_first), (z1, z_second)):
         big, small = parts_of(which, 2)
         ref[0:NRHS, :] = big
@@ -334,11 +351,11 @@
 
                 @pl.when(position == 0)
                 def _():
-                    result[0] = y_first[...]
+                    result[0] = y_first[...].T
 
                 @pl.when(position == 1)
                 def _():
-                    result[0] = y_second[...]
+                    result[0] = y_second[...].T
 
             store = pltpu.make_async_copy(result.at[t], out.at[t, 0], out_sems.at[t])
             store.start()
@@ -384,46 +401,47 @@
     params = pltpu.CompilerParams(vmem_limit_bytes=12 << 20)
     estimate = pl.CostEstimate(flops=4 * 10**9, bytes_accessed=10**6, transcendentals=0)
     strip = [pltpu.VMEM((size, LANES), f32)]
-    inverse, diagonal, packed = pl.pallas_call(
-        first_kernel,
-        out_shape=[square, stack, jax.ShapeDtypeStruct((packed_size, breadth), bf16)],
-        in_specs=[pl.BlockSpec(memory_space=pltpu.HBM)] * 5,
-        out_specs=[whole, anywhere, whole],
-        scratch_shapes=strip
-        + room
-        + [
-            pltpu.VMEM(points.shape, jnp.int32),
+    hbm = pl.BlockSpec(memory_space=pltpu.HBM)
+
+    def stay(*arrays):
+        return tuple(pltpu.with_memory_space_constraint(x, pltpu.HBM) for x in arrays)
+
+    got = pl.pallas_call(
+        pack_kernel,
+        out_shape=jax.ShapeDtypeStruct((packed_size, breadth), bf16),
+        in_specs=[hbm] * 4,
+        out_specs=whole,
+        scratch_shapes=[
             pltpu.SMEM(rank_rows.shape, jnp.int32),
             pltpu.VMEM((1, size), jnp.int32),
             pltpu.VMEM((size, breadth), bf16),
             pltpu.VMEM((size, breadth), bf16),
-            pltpu.SemaphoreType.DMA,
-            pltpu.SemaphoreType.DMA((5,)),
+            pltpu.SemaphoreType.DMA((4,)),
         ],
-        compiler_params=params,
-        cost_estimate=estimate,
-        name="first0",
-    )(*(pltpu.with_memory_space_constraint(x, pltpu.HBM) for x in (points, rank_rows, labels, u_first, v_first)))
-    got = packed
+        compiler_params=pltpu.CompilerParams(vmem_limit_bytes=8 << 20),
+        name="pack",
+    )(*stay(rank_rows, labels, u_first, v_first))
     pairs = hops(row_size)
-    for k in range(1, blocks):
-        late = lax.ppermute(got, "row", pairs[k - 1]) if k < len(pairs) else None
+    for k in range(blocks):
+        late = lax.ppermute(got, "row", pairs[k]) if k < len(pairs) - 1 else None
         inverse, diagonal = pl.pallas_call(
-            functools.partial(next_kernel, k),
+            functools.partial(next_kernel, k) if k else first_kernel,
             out_shape=[square, stack],
-            in_specs=[whole, anywhere],
+            in_specs=[whole, anywhere] if k else [hbm],
             out_specs=[whole, anywhere],
-            input_output_aliases={0: 0, 1: 1},
-            scratch_shapes=strip + room + [pltpu.SemaphoreType.DMA],
+            input_output_aliases={0: 0, 1: 1} if k else {},
+            scratch_shapes=strip
+            + room
+            + ([] if k else [pltpu.VMEM(points.shape, jnp.int32)])
+            + [pltpu.SemaphoreType.DMA],
             compiler_params=params,
             cost_estimate=estimate,
             name=f"first{k}",
-        )(inverse, diagonal)
+        )(*((inverse, diagonal) if k else stay(points)))
         if late is not None:
             late, inverse = lax.optimization_barrier((late, inverse))
             got = got + late
-
-    for pair in pairs[blocks - 1 : -1]:
+    for pair in pairs[blocks:-1]:
         got = got + lax.ppermute(got, "row", pair)
     came = lax.ppermute(got, "row", pairs[-1])
 
@@ -436,8 +454,8 @@
             pltpu.VMEM((size, size), f32),
             pltpu.VMEM((blocks, size, LANES), f32),
             *room,
-            pltpu.VMEM((size, NRHS), f32),
-            pltpu.VMEM((size, NRHS), f32),
+            pltpu.VMEM((NRHS, size), f32),
+            pltpu.VMEM((NRHS, size), f32),
             pltpu.VMEM((2 * NRHS, size), bf16),
             pltpu.VMEM((2 * NRHS, size), bf16),
             pltpu.VMEM((cycles, size, NRHS), f32),

time: 53.8 us -> 52.8 us (0.981)
  Pallas kernels: 39.7 us -> 41.7 us
  waiting for transfers between devices: 3.78 us -> 1.94 us
  starting transfers between devices: 8.19 us -> 7.19 us
    ppermute x1, waiting for transfers between devices: 1.53 us -> 0.01 us  [local(): came = lax.ppermute(got, 'row', pairs[-1])]
    pallas_call x1, Pallas kernels: 22.3 us -> 23.3 us  [local(): pl.pallas_call(second_kernel, out_shape=[stack, jax.ShapeDtypeStruct((cyc...]
    ppermute x3, starting transfers between devices: 8.12 us -> 7.12 us  [local(): late = lax.ppermute(got, 'row', pairs[k]) if k < len(pairs) - 1 else None]
    pallas_call x4 -> x5, Pallas kernels: 17.4 us -> 18.3 us  [the longest x4 17.2 us: local(): pl.pallas_call(functools.partial(next_kernel, k) if k else first_kernel,...]
  transfers between devices with their start and end apart: 4 -> 4, of which waited for: 2 -> 1; matrix products, arithmetic and copies ran while one was open for 0% -> 0% of each run, Pallas kernels for 22% -> 33%
where the time goes in v5:
time: 52.8 us; the launch traced here: 52.1 us
  Pallas kernels  41.7 us (79%)
  starting transfers between devices  7.19 us (14%)
  waiting for transfers between devices  1.94 us (4%)
  between operations  1.03 us (2%)
    pallas_call x1, Pallas kernels, local(): pl.pallas_call(second_kernel, out_shape=[stack, jax.ShapeDtypeStruct((cyc...  23.3 us
    pallas_call x4, Pallas kernels, local(): pl.pallas_call(functools.partial(next_kernel, k) if k else first_kernel,...  17.2 us
    ppermute x3, starting transfers between devices, local(): late = lax.ppermute(got, 'row', pairs[k]) if k < len(pairs) - 1 else None  7.12 us
    ppermute x3, waiting for transfers between devices, local(): late = lax.ppermute(got, 'row', pairs[k]) if k < len(pairs) - 1 else None  1.94 us
    pallas_call x1, Pallas kernels, local(): pl.pallas_call(pack_kernel, out_shape=jax.ShapeDtypeStruct((packed_size,...  1.09 us
  transfers between devices with their start and end apart: 4, of which 1 were waited for; matrix products, arithmetic and copies ran while one was open for 0% of the time, Pallas kernels for 33%

profile of v5, /device:TPU:0, one launch (start us, length us, event | category | flops | bytes accessed | tf_op | source)
XLA Modules:
  0.0 52.1 jit_solution(17762433820502098602)
XLA Ops:
  0.6 1.1 %pack.1 = bf16[1040,128]{1,0:T(8,128)(2,1)S(1)} custom-call(s32[2,8]{1,0:T(2,128)} %bitcast.6, s32[8,1,512]{2,1,0:T(1,128)} %label_rows.1, bf16[8,1,512,128]{3,2,1,0:T(8,128)(2,1)} %u0.1, bf16[8,1,512,128]{3,2,1,0:T(8,128)(2,1)} %v0.1), custom_call_target="tpu_custom_call" | custom-call | tf_op jit(solution)/shard_map/pack/pallas_call | solution.py:409
  1.7 3.9 %collective-permute-start = (bf16[1040,128]{1,0:T(8,128)(2,1)S(1)}, bf16[1040,128]{1,0:T(8,128)(2,1)S(1)}, u32[]{:S(2)}, u32[]{:S(2)}) collective-permute-start(bf16[1040,128]{1,0:T(8,128)(2,1)S(1)} %pack.1), channel_id=1, source_target_pairs={{1,9},{0,2},{17,25},{16,18}} | collective-permute-start | bytes 798728 | tf_op jit(solution)/shard_map/ppermute | solution.py:426
  5.6 5.3 %first0.1 = (f32[512,512]{1,0:T(8,128)S(1)}, f32[2,512,512]{2,1,0:T(8,128)}) custom-call(s32[3,2,512]{2,1,0:T(2,128)} %bitcast.4), custom_call_target="tpu_custom_call" | custom-call | flops 4000000000 | bytes 1000000 | tf_op jit(solution)/shard_map/first0/pallas_call | solution.py:427
  10.9 0.0 collective-permute-done
  11.0 0.1 add.9
  11.0 1.8 %collective-permute-start.1 = (bf16[1040,128]{1,0:T(8,128)(2,1)S(1)}, bf16[1040,128]{1,0:T(8,128)(2,1)S(1)}, u32[]{:S(2)}, u32[]{:S(2)}) collective-permute-start(bf16[1040,128]{1,0:T(8,128)(2,1)S(1)} %add.9), channel_id=1, source_target_pairs={{1,5},{9,13},{0,8},{2,10},{17,21},{25,29},{16,24},{18,26}} | collective-permute-start | bytes 798728 | tf_op jit(solution)/shard_map/ppermute | solution.py:426
  12.8 4.3 %first1.1 = (f32[512,512]{1,0:T(8,128)S(1)}, f32[2,512,512]{2,1,0:T(8,128)}) custom-call(f32[512,512]{1,0:T(8,128)S(1)} %get-tuple-element.20.old, f32[2,512,512]{2,1,0:T(8,128)} %get-tuple-element.21._), custom_call_target="tpu_custom_call", output_to_operand_aliasing={{0}: (0, {}), {1}: (1, {})} | custom-call | flops 4000000000 | bytes 1000000 | tf_op jit(solution)/shard_map/first1/pallas_call | solution.py:427
  17.1 1.9 %collective-permute-done.1 = bf16[1040,128]{1,0:T(8,128)(2,1)S(1)} collective-permute-done((bf16[1040,128]{1,0:T(8,128)(2,1)S(1)}, bf16[1040,128]{1,0:T(8,128)(2,1)S(1)}, u32[]{:S(2)}, u32[]{:S(2)}) %collective-permute-start.1) | collective-permute-done | bytes 266272 | tf_op jit(solution)/shard_map/ppermute | solution.py:426
  19.0 0.1 add.10
  19.1 1.5 %collective-permute-start.2 = (bf16[1040,128]{1,0:T(8,128)(2,1)S(1)}, bf16[1040,128]{1,0:T(8,128)(2,1)S(1)}, u32[]{:S(2)}, u32[]{:S(2)}) collective-permute-start(bf16[1040,128]{1,0:T(8,128)(2,1)S(1)} %add.10), channel_id=1, source_target_pairs={{1,3},{9,11},{5,7},{13,15},{0,4},{2,6},{8,12},{10,14},{17,19},{25,... | collective-permute-start | bytes 798728 | tf_op jit(solution)/shard_map/ppermute | solution.py:426
  20.6 4.0 %first2.1 = (f32[512,512]{1,0:T(8,128)S(1)}, f32[2,512,512]{2,1,0:T(8,128)}) custom-call(f32[512,512]{1,0:T(8,128)S(1)} %get-tuple-element.24.old, f32[2,512,512]{2,1,0:T(8,128)} %get-tuple-element.25._), custom_call_target="tpu_custom_call", output_to_operand_aliasing={{0}: (0, {}), {1}: (1, {})} | custom-call | flops 4000000000 | bytes 1000000 | tf_op jit(solution)/shard_map/first2/pallas_call | solution.py:427
  24.6 0.0 collective-permute-done.2
  24.6 0.1 add.11.got
  24.7 0.1 collective-permute-start.3
  24.8 0.0 copy-start
  24.8 0.0 copy-start.1
  24.8 0.0 copy-start.2
  24.8 0.0 copy-start.3
  24.8 0.0 copy-start.4
  24.8 0.0 copy-start.5
  24.9 0.0 copy-start.6
  24.9 3.6 %first3.1 = (f32[512,512]{1,0:T(8,128)S(1)}, f32[2,512,512]{2,1,0:T(8,128)}) custom-call(f32[512,512]{1,0:T(8,128)S(1)} %get-tuple-element.28.old, f32[2,512,512]{2,1,0:T(8,128)} %get-tuple-element.29._), custom_call_target="tpu_custom_call", output_to_operand_aliasing={{0}: (0, {}), {1}: (1, {})} | custom-call | flops 4000000000 | bytes 1000000 | tf_op jit(solution)/shard_map/first3/pallas_call | solution.py:427
  28.5 0.0 collective-permute-done.3.came
  28.5 0.0 copy-done
  28.5 0.0 copy-done.1
  28.5 0.0 copy-done.2
  28.5 0.0 copy-done.3
  28.5 0.0 copy-done.4
  28.6 0.0 copy-done.5
  28.6 0.0 copy-done.6
  28.6 23.3 %second.1 = (f32[2,512,512]{2,1,0:T(8,128)}, f32[8,1,512,256]{3,2,1,0:T(8,128)}) custom-call(s32[3,2,512]{2,1,0:T(2,128)S(1)} %bitcast.5, s32[2,8]{1,0:T(2,128)S(1)} %bitcast.7, s32[8,1,512]{2,1,0:T(1,128)S(1)} %copy-done.4, bf16[1040,128]{1,0:T(8,128)(2,1)S(1)} %add.11.got, ...), custom_call_target="tpu_custom_call", output_to_operand_aliasing={{0}: (10, {})} | custom-call | tf_op jit(solution)/shard_map/second/pallas_call | solution.py:448
Async XLA Ops:
  1.7 9.2 %collective-permute-start = (bf16[1040,128]{1,0:T(8,128)(2,1)S(1)}, bf16[1040,128]{1,0:T(8,128)(2,1)S(1)}, u32[]{:S(2)}, u32[]{:S(2)}) collective-permute-start(bf16[1040,128]{1,0:T(8,128)(2,1)S(1)} %pack.1), channel_id=1, source_target_pairs={{1,9},{0,2},{17,25},{16,18}} | collective-permute-start | bytes 798728 | tf_op jit(solution)/shard_map/ppermute | solution.py:426
  11.0 8.0 %collective-permute-start.1 = (bf16[1040,128]{1,0:T(8,128)(2,1)S(1)}, bf16[1040,128]{1,0:T(8,128)(2,1)S(1)}, u32[]{:S(2)}, u32[]{:S(2)}) collective-permute-start(bf16[1040,128]{1,0:T(8,128)(2,1)S(1)} %add.9), channel_id=1, source_target_pairs={{1,5},{9,13},{0,8},{2,10},{17,21},{25,29},{16,24},{18,26}} | collective-permute-start | bytes 798728 | tf_op jit(solution)/shard_map/ppermute | solution.py:426
  19.1 5.5 %collective-permute-start.2 = (bf16[1040,128]{1,0:T(8,128)(2,1)S(1)}, bf16[1040,128]{1,0:T(8,128)(2,1)S(1)}, u32[]{:S(2)}, u32[]{:S(2)}) collective-permute-start(bf16[1040,128]{1,0:T(8,128)(2,1)S(1)} %add.10), channel_id=1, source_target_pairs={{1,3},{9,11},{5,7},{13,15},{0,4},{2,6},{8,12},{10,14},{17,19},{25,... | collective-permute-start | bytes 798728 | tf_op jit(solution)/shard_map/ppermute | solution.py:426
  24.7 3.8 %collective-permute-start.3 = (bf16[1040,128]{1,0:T(8,128)(2,1)S(1)}, bf16[1040,128]{1,0:T(8,128)(2,1)S(1)}, u32[]{:S(2)}, u32[]{:S(2)}) collective-permute-start(bf16[1040,128]{1,0:T(8,128)(2,1)S(1)} %add.11.got), channel_id=1, source_target_pairs={{0,1},{1,0},{2,3},{3,2},{4,5},{5,4},{6,7},{7,6},{8,9},{9,8},{10,11... | collective-permute-start | bytes 798728 | tf_op jit(solution)/shard_map/ppermute | solution.py:446
  24.8 3.7 %copy-start = (bf16[8,1,512,128]{3,2,1,0:T(8,128)(2,1)S(1)}, bf16[8,1,512,128]{3,2,1,0:T(8,128)(2,1)}, u32[]{:S(2)}) copy-start(bf16[8,1,512,128]{3,2,1,0:T(8,128)(2,1)} %u0.1) | copy-start | bytes 3145732
  24.8 3.7 %copy-start.1 = (bf16[8,1,512,128]{3,2,1,0:T(8,128)(2,1)S(1)}, bf16[8,1,512,128]{3,2,1,0:T(8,128)(2,1)}, u32[]{:S(2)}) copy-start(bf16[8,1,512,128]{3,2,1,0:T(8,128)(2,1)} %v0.1) | copy-start | bytes 3145732
  24.8 3.7 %copy-start.2 = (bf16[8,1,512,128]{3,2,1,0:T(8,128)(2,1)S(1)}, bf16[8,1,512,128]{3,2,1,0:T(8,128)(2,1)}, u32[]{:S(2)}) copy-start(bf16[8,1,512,128]{3,2,1,0:T(8,128)(2,1)} %u1_.1) | copy-start | bytes 3145732
  24.8 3.7 %copy-start.3 = (bf16[8,1,512,128]{3,2,1,0:T(8,128)(2,1)S(1)}, bf16[8,1,512,128]{3,2,1,0:T(8,128)(2,1)}, u32[]{:S(2)}) copy-start(bf16[8,1,512,128]{3,2,1,0:T(8,128)(2,1)} %v1.1) | copy-start | bytes 3145732
  24.8 3.7 %copy-start.4 = (s32[8,1,512]{2,1,0:T(1,128)S(1)}, s32[8,1,512]{2,1,0:T(1,128)}, u32[]{:S(2)}) copy-start(s32[8,1,512]{2,1,0:T(1,128)} %label_rows.1) | copy-start | bytes 49156
  24.8 3.7 %copy-start.5 = (s32[2,3,512]{2,0,1:T(2,128)S(1)}, s32[2,3,512]{2,0,1:T(2,128)}, u32[]{:S(2)}) copy-start(s32[2,3,512]{2,0,1:T(2,128)} %param.7) | copy-start | bytes 36868
  24.9 3.7 %copy-start.6 = (s32[8,1,2]{0,2,1:T(2,128)S(1)}, s32[8,1,2]{0,2,1:T(2,128)}, u32[]{:S(2)}) copy-start(s32[8,1,2]{0,2,1:T(2,128)} %param.9) | copy-start | bytes 196

commit v6 on v5

--- a/solution.py
+++ b/solution.py
@@ -161,8 +161,8 @@
                 rows[i] = jnp.where(here, 0.0, rows[i]) - update
 
 
-def factor_step(matrix, strip, corner, panel, k):
-    size = matrix.shape[0]
+def factor_step(matrix, strip, corner, panel, k, send):
+    size, wide = matrix.shape
     low, top = LANES * k, LANES * (k + 1)
 
     def put(step, upper_rows, inverse_rows):
@@ -174,19 +174,21 @@
         [matrix[low + SUB * i : low + SUB * (i + 1), low:top] for i in range(LANES // SUB)], put
     )
     own = panel[:, low:top]
+    if top < wide:
+        panel[:, top:] = mul(own, matrix[low:top, top:], NN, highest)
     if low:
         strip[:low, :] = jnp.zeros((low, LANES), f32)
+    strip[low:top, :] = corner[...].T
+    for i in range(top, size, LANES):
+        strip[i : i + LANES, :] = panel[:, i : i + LANES].T
+    send()
+    if low:
         panel[:, :low] = mul(own, matrix[low:top, :low], NN, highest)
-        matrix[low:top, :low] = panel[:, :low]
-    strip[low:top, :] = corner[...].T
-    matrix[low:top, low:top] = own
     if top < size:
-        panel[:, top:] = mul(own, matrix[low:top, top:], NN, highest)
-        matrix[low:top, top:] = jnp.zeros((LANES, size - top), f32)
-        for i in range(top, size, LANES):
-            strip[i : i + LANES, :] = panel[:, i : i + LANES].T
         matrix[top:, low:top] = jnp.zeros((size - top, LANES), f32)
         matrix[top:, :] = matrix[top:, :] - mul(strip[top:, :], panel[...], NN, highest)
+        matrix[low:top, top:size] = jnp.zeros((LANES, size - top), f32)
+    matrix[low:top, :top] = panel[:, :top]
 
 
 def kernel_tile(points):
@@ -268,9 +270,8 @@
 
 
 def first_step(k, matrix, diagonal, strip, corner, panel, sem):
-    factor_step(matrix, strip, corner, panel, k)
     copy = pltpu.make_async_copy(strip, diagonal.at[0, :, pl.ds(LANES * k, LANES)], sem)
-    copy.start()
+    factor_step(matrix, strip, corner, panel, k, copy.start)
     copy.wait()
 
 
@@ -293,28 +294,35 @@
             [labels[which * spread + i : which * spread + i + 1, :] for i in range(spread)], axis=1
         )
 
-    first_b = onehot_rows(label_row(0)).astype(bf16)
     w_one = lower_left(split_left, inverse[...], v_one)
     w_flat = w_one.T
     gram = mul(w_flat, w_one, NN, highest)
     left = split_right(u_one, gram)
-    matrix[...] = kernel_tile(coords[:, 1, :]) - split_left(left, u_one, NT)
-    y0 = right_upper(split_right, first_b, inverse)
+    matrix[:, :size] = kernel_tile(coords[:, 1, :]) - split_left(left, u_one, NT)
+    y0 = right_upper(split_right, onehot_rows(label_row(0)).astype(bf16), inverse)
     y_first[...] = y0
-    target = onehot_rows(label_row(1)) - split_left(mul(y0, w_one, NN, highest), u_one, NT)
+    lane = lax.broadcasted_iota(jnp.int32, (size, LANES), 1).astype(f32)
+
+    def onehot(column):
+        return jnp.concatenate(
+            [jnp.where(column == lane + float(LANES * j), 1.0, 0.0) for j in range(NRHS // LANES)],
+            axis=1,
+        )
+
+    own_column = jnp.broadcast_to(label_row(1), (LANES, size)).T
+    weights_one = mul(y0, w_one, NN, highest).T
+    matrix[:, size:] = onehot(own_column) - split_right(u_one, weights_one)
     z0 = right_lower(y0, inverse)
     p_one = right_lower(w_flat, inverse)
     strips = []
     for k in range(size // LANES):
-        factor_step(matrix, strip.at[k], corner, panel, k)
         copy = pltpu.make_async_copy(
             strip.at[k], diagonal.at[1, :, pl.ds(LANES * k, LANES)], strip_sems.at[k]
         )
-        copy.start()
+        factor_step(matrix, strip.at[k], corner, panel, k, copy.start)
+        y_second[:, LANES * k : LANES * (k + 1)] = panel[:, size:].T
         strips.append(copy)
-    y1 = right_upper(functools.partial(mul, precision=high), target, matrix)
-    y_second[...] = y1
-    z1 = right_lower(y1, matrix)
+    z1 = right_lower(y_second[...], matrix.at[:, :size])
     q_one = split_left(z1, u_one, NN, 2)
     zc = z0 - mul(q_one, p_one, NN, high)
     for which, ref in ((zc, z_first), (z1, z_second)):
@@ -322,7 +330,6 @@
         ref[0:NRHS, :] = big
         ref[NRHS:, :] = small
     columns = label_rows[:, 0, :].astype(f32).T
-    lane = lax.broadcasted_iota(jnp.int32, (size, LANES), 1).astype(f32)
     keep = lax.broadcasted_iota(jnp.int32, (NRHS, LANES), 1)
     position = lax.axis_index("row")
     stores = []
@@ -342,11 +349,7 @@
             both = jnp.concatenate([h_first[i], h_second[i]], axis=1)
             total = split_right(jnp.concatenate([u0[t, 0], u1[t, 0]], axis=1), both, NT, 2)
             column = jnp.broadcast_to(columns[:, t : t + 1], (size, LANES))
-            hot = jnp.concatenate(
-                [jnp.where(column == lane + float(LANES * j), 1.0, 0.0) for j in range(NRHS // LANES)],
-                axis=1,
-            )
-            result[t] = hot - total
+            result[t] = onehot(column) - total
             if t == 0:
 
                 @pl.when(position == 0)
@@ -451,9 +454,10 @@
         in_specs=[whole, scalars] + [whole] * 8 + [anywhere],
         out_specs=[anywhere, anywhere],
         scratch_shapes=[
-            pltpu.VMEM((size, size), f32),
+            pltpu.VMEM((size, size + NRHS), f32),
             pltpu.VMEM((blocks, size, LANES), f32),
-            *room,
+            pltpu.VMEM((LANES, LANES), f32),
+            pltpu.VMEM((LANES, size + NRHS), f32),
             pltpu.VMEM((NRHS, size), f32),
             pltpu.VMEM((NRHS, size), f32),
             pltpu.VMEM((2 * NRHS, size), bf16),

time: 52.8 us -> 52.6 us (level)
  no operation moved by 1% of the time
where the time goes in v6:
time: 52.6 us; the launch traced here: 51.9 us
  Pallas kernels  41.5 us (79%)
  starting transfers between devices  7.19 us (14%)
  waiting for transfers between devices  1.93 us (4%)
  between operations  1.03 us (2%)
    pallas_call x1, Pallas kernels, local(): pl.pallas_call(second_kernel, out_shape=[stack, jax.ShapeDtypeStruct((cyc...  23.2 us
    pallas_call x4, Pallas kernels, local(): pl.pallas_call(functools.partial(next_kernel, k) if k else first_kernel,...  17.2 us
    ppermute x3, starting transfers between devices, local(): late = lax.ppermute(got, 'row', pairs[k]) if k < len(pairs) - 1 else None  7.12 us
    ppermute x3, waiting for transfers between devices, local(): late = lax.ppermute(got, 'row', pairs[k]) if k < len(pairs) - 1 else None  1.92 us
    pallas_call x1, Pallas kernels, local(): pl.pallas_call(pack_kernel, out_shape=jax.ShapeDtypeStruct((packed_size,...  1.09 us
  transfers between devices with their start and end apart: 4, of which 1 were waited for; matrix products, arithmetic and copies ran while one was open for 0% of the time, Pallas kernels for 33%

profile of v6, /device:TPU:0, one launch (start us, length us, event | category | flops | bytes accessed | tf_op | source)
XLA Modules:
  0.0 51.9 jit_solution(5676649561699186782)
XLA Ops:
  0.6 1.1 %pack.1 = bf16[1040,128]{1,0:T(8,128)(2,1)S(1)} custom-call(s32[2,8]{1,0:T(2,128)} %bitcast.6, s32[8,1,512]{2,1,0:T(1,128)} %label_rows.1, bf16[8,1,512,128]{3,2,1,0:T(8,128)(2,1)} %u0.1, bf16[8,1,512,128]{3,2,1,0:T(8,128)(2,1)} %v0.1), custom_call_target="tpu_custom_call" | custom-call | tf_op jit(solution)/shard_map/pack/pallas_call | solution.py:412
  1.7 3.9 %collective-permute-start = (bf16[1040,128]{1,0:T(8,128)(2,1)S(1)}, bf16[1040,128]{1,0:T(8,128)(2,1)S(1)}, u32[]{:S(2)}, u32[]{:S(2)}) collective-permute-start(bf16[1040,128]{1,0:T(8,128)(2,1)S(1)} %pack.1), channel_id=1, source_target_pairs={{1,9},{0,2},{17,25},{16,18}} | collective-permute-start | bytes 798728 | tf_op jit(solution)/shard_map/ppermute | solution.py:429
  5.6 5.3 %first0.1 = (f32[512,512]{1,0:T(8,128)S(1)}, f32[2,512,512]{2,1,0:T(8,128)}) custom-call(s32[3,2,512]{2,1,0:T(2,128)} %bitcast.4), custom_call_target="tpu_custom_call" | custom-call | flops 4000000000 | bytes 1000000 | tf_op jit(solution)/shard_map/first0/pallas_call | solution.py:430
  10.9 0.0 collective-permute-done
  11.0 0.1 add.9
  11.0 1.8 %collective-permute-start.1 = (bf16[1040,128]{1,0:T(8,128)(2,1)S(1)}, bf16[1040,128]{1,0:T(8,128)(2,1)S(1)}, u32[]{:S(2)}, u32[]{:S(2)}) collective-permute-start(bf16[1040,128]{1,0:T(8,128)(2,1)S(1)} %add.9), channel_id=1, source_target_pairs={{1,5},{9,13},{0,8},{2,10},{17,21},{25,29},{16,24},{18,26}} | collective-permute-start | bytes 798728 | tf_op jit(solution)/shard_map/ppermute | solution.py:429
  12.8 4.3 %first1.1 = (f32[512,512]{1,0:T(8,128)S(1)}, f32[2,512,512]{2,1,0:T(8,128)}) custom-call(f32[512,512]{1,0:T(8,128)S(1)} %get-tuple-element.20.old, f32[2,512,512]{2,1,0:T(8,128)} %get-tuple-element.21._), custom_call_target="tpu_custom_call", output_to_operand_aliasing={{0}: (0, {}), {1}: (1, {})} | custom-call | flops 4000000000 | bytes 1000000 | tf_op jit(solution)/shard_map/first1/pallas_call | solution.py:430
  17.1 1.9 %collective-permute-done.1 = bf16[1040,128]{1,0:T(8,128)(2,1)S(1)} collective-permute-done((bf16[1040,128]{1,0:T(8,128)(2,1)S(1)}, bf16[1040,128]{1,0:T(8,128)(2,1)S(1)}, u32[]{:S(2)}, u32[]{:S(2)}) %collective-permute-start.1) | collective-permute-done | bytes 266272 | tf_op jit(solution)/shard_map/ppermute | solution.py:429
  19.0 0.1 add.10
  19.1 1.5 %collective-permute-start.2 = (bf16[1040,128]{1,0:T(8,128)(2,1)S(1)}, bf16[1040,128]{1,0:T(8,128)(2,1)S(1)}, u32[]{:S(2)}, u32[]{:S(2)}) collective-permute-start(bf16[1040,128]{1,0:T(8,128)(2,1)S(1)} %add.10), channel_id=1, source_target_pairs={{1,3},{9,11},{5,7},{13,15},{0,4},{2,6},{8,12},{10,14},{17,19},{25,... | collective-permute-start | bytes 798728 | tf_op jit(solution)/shard_map/ppermute | solution.py:429
  20.6 4.0 %first2.1 = (f32[512,512]{1,0:T(8,128)S(1)}, f32[2,512,512]{2,1,0:T(8,128)}) custom-call(f32[512,512]{1,0:T(8,128)S(1)} %get-tuple-element.24.old, f32[2,512,512]{2,1,0:T(8,128)} %get-tuple-element.25._), custom_call_target="tpu_custom_call", output_to_operand_aliasing={{0}: (0, {}), {1}: (1, {})} | custom-call | flops 4000000000 | bytes 1000000 | tf_op jit(solution)/shard_map/first2/pallas_call | solution.py:430
  24.6 0.0 collective-permute-done.2
  24.6 0.1 add.11.got
  24.7 0.1 collective-permute-start.3
  24.8 0.0 copy-start
  24.8 0.0 copy-start.1
  24.8 0.0 copy-start.2
  24.8 0.0 copy-start.3
  24.8 0.0 copy-start.4
  24.8 0.0 copy-start.5
  24.8 0.0 copy-start.6
  24.9 3.6 %first3.1 = (f32[512,512]{1,0:T(8,128)S(1)}, f32[2,512,512]{2,1,0:T(8,128)}) custom-call(f32[512,512]{1,0:T(8,128)S(1)} %get-tuple-element.28.old, f32[2,512,512]{2,1,0:T(8,128)} %get-tuple-element.29._), custom_call_target="tpu_custom_call", output_to_operand_aliasing={{0}: (0, {}), {1}: (1, {})} | custom-call | flops 4000000000 | bytes 1000000 | tf_op jit(solution)/shard_map/first3/pallas_call | solution.py:430
  28.5 0.0 collective-permute-done.3.came
  28.5 0.0 copy-done
  28.5 0.0 copy-done.1
  28.5 0.0 copy-done.2
  28.5 0.0 copy-done.3
  28.5 0.0 copy-done.4
  28.5 0.0 copy-done.5
  28.6 0.0 copy-done.6
  28.6 23.2 %second.1 = (f32[2,512,512]{2,1,0:T(8,128)}, f32[8,1,512,256]{3,2,1,0:T(8,128)}) custom-call(s32[3,2,512]{2,1,0:T(2,128)S(1)} %bitcast.5, s32[2,8]{1,0:T(2,128)S(1)} %bitcast.7, s32[8,1,512]{2,1,0:T(1,128)S(1)} %copy-done.4, bf16[1040,128]{1,0:T(8,128)(2,1)S(1)} %add.11.got, ...), custom_call_target="tpu_custom_call", output_to_operand_aliasing={{0}: (10, {})} | custom-call | tf_op jit(solution)/shard_map/second/pallas_call | solution.py:451
Async XLA Ops:
  1.7 9.2 %collective-permute-start = (bf16[1040,128]{1,0:T(8,128)(2,1)S(1)}, bf16[1040,128]{1,0:T(8,128)(2,1)S(1)}, u32[]{:S(2)}, u32[]{:S(2)}) collective-permute-start(bf16[1040,128]{1,0:T(8,128)(2,1)S(1)} %pack.1), channel_id=1, source_target_pairs={{1,9},{0,2},{17,25},{16,18}} | collective-permute-start | bytes 798728 | tf_op jit(solution)/shard_map/ppermute | solution.py:429
  11.0 8.0 %collective-permute-start.1 = (bf16[1040,128]{1,0:T(8,128)(2,1)S(1)}, bf16[1040,128]{1,0:T(8,128)(2,1)S(1)}, u32[]{:S(2)}, u32[]{:S(2)}) collective-permute-start(bf16[1040,128]{1,0:T(8,128)(2,1)S(1)} %add.9), channel_id=1, source_target_pairs={{1,5},{9,13},{0,8},{2,10},{17,21},{25,29},{16,24},{18,26}} | collective-permute-start | bytes 798728 | tf_op jit(solution)/shard_map/ppermute | solution.py:429
  19.1 5.5 %collective-permute-start.2 = (bf16[1040,128]{1,0:T(8,128)(2,1)S(1)}, bf16[1040,128]{1,0:T(8,128)(2,1)S(1)}, u32[]{:S(2)}, u32[]{:S(2)}) collective-permute-start(bf16[1040,128]{1,0:T(8,128)(2,1)S(1)} %add.10), channel_id=1, source_target_pairs={{1,3},{9,11},{5,7},{13,15},{0,4},{2,6},{8,12},{10,14},{17,19},{25,... | collective-permute-start | bytes 798728 | tf_op jit(solution)/shard_map/ppermute | solution.py:429
  24.7 3.8 %collective-permute-start.3 = (bf16[1040,128]{1,0:T(8,128)(2,1)S(1)}, bf16[1040,128]{1,0:T(8,128)(2,1)S(1)}, u32[]{:S(2)}, u32[]{:S(2)}) collective-permute-start(bf16[1040,128]{1,0:T(8,128)(2,1)S(1)} %add.11.got), channel_id=1, source_target_pairs={{0,1},{1,0},{2,3},{3,2},{4,5},{5,4},{6,7},{7,6},{8,9},{9,8},{10,11... | collective-permute-start | bytes 798728 | tf_op jit(solution)/shard_map/ppermute | solution.py:449
  24.8 3.7 %copy-start = (bf16[8,1,512,128]{3,2,1,0:T(8,128)(2,1)S(1)}, bf16[8,1,512,128]{3,2,1,0:T(8,128)(2,1)}, u32[]{:S(2)}) copy-start(bf16[8,1,512,128]{3,2,1,0:T(8,128)(2,1)} %u0.1) | copy-start | bytes 3145732
  24.8 3.7 %copy-start.1 = (bf16[8,1,512,128]{3,2,1,0:T(8,128)(2,1)S(1)}, bf16[8,1,512,128]{3,2,1,0:T(8,128)(2,1)}, u32[]{:S(2)}) copy-start(bf16[8,1,512,128]{3,2,1,0:T(8,128)(2,1)} %v0.1) | copy-start | bytes 3145732
  24.8 3.7 %copy-start.2 = (bf16[8,1,512,128]{3,2,1,0:T(8,128)(2,1)S(1)}, bf16[8,1,512,128]{3,2,1,0:T(8,128)(2,1)}, u32[]{:S(2)}) copy-start(bf16[8,1,512,128]{3,2,1,0:T(8,128)(2,1)} %u1_.1) | copy-start | bytes 3145732
  24.8 3.7 %copy-start.3 = (bf16[8,1,512,128]{3,2,1,0:T(8,128)(2,1)S(1)}, bf16[8,1,512,128]{3,2,1,0:T(8,128)(2,1)}, u32[]{:S(2)}) copy-start(bf16[8,1,512,128]{3,2,1,0:T(8,128)(2,1)} %v1.1) | copy-start | bytes 3145732
  24.8 3.7 %copy-start.4 = (s32[8,1,512]{2,1,0:T(1,128)S(1)}, s32[8,1,512]{2,1,0:T(1,128)}, u32[]{:S(2)}) copy-start(s32[8,1,512]{2,1,0:T(1,128)} %label_rows.1) | copy-start | bytes 49156
  24.8 3.7 %copy-start.5 = (s32[2,3,512]{2,0,1:T(2,128)S(1)}, s32[2,3,512]{2,0,1:T(2,128)}, u32[]{:S(2)}) copy-start(s32[2,3,512]{2,0,1:T(2,128)} %param.7) | copy-start | bytes 36868
  24.8 3.7 %copy-start.6 = (s32[8,1,2]{0,2,1:T(2,128)S(1)}, s32[8,1,2]{0,2,1:T(2,128)}, u32[]{:S(2)}) copy-start(s32[8,1,2]{0,2,1:T(2,128)} %param.9) | copy-start | bytes 196

commit v7 on v6

--- a/solution.py
+++ b/solution.py
@@ -175,7 +175,7 @@
     )
     own = panel[:, low:top]
     if top < wide:
-        panel[:, top:] = mul(own, matrix[low:top, top:], NN, highest)
+        panel[:, top:] = mul(own, matrix[low:top, top:], NN, high)
     if low:
         strip[:low, :] = jnp.zeros((low, LANES), f32)
     strip[low:top, :] = corner[...].T
@@ -183,10 +183,10 @@
         strip[i : i + LANES, :] = panel[:, i : i + LANES].T
     send()
     if low:
-        panel[:, :low] = mul(own, matrix[low:top, :low], NN, highest)
+        panel[:, :low] = mul(own, matrix[low:top, :low], NN, high)
     if top < size:
         matrix[top:, low:top] = jnp.zeros((size - top, LANES), f32)
-        matrix[top:, :] = matrix[top:, :] - mul(strip[top:, :], panel[...], NN, highest)
+        matrix[top:, :] = matrix[top:, :] - mul(strip[top:, :], panel[...], NN, high)
         matrix[low:top, top:size] = jnp.zeros((LANES, size - top), f32)
     matrix[low:top, :top] = panel[:, :top]
 

time: 52.6 us -> 51 us (0.970)
  Pallas kernels: 41.5 us -> 39.2 us
    pallas_call x4, Pallas kernels: 17.2 us -> 16.1 us  [local(): pl.pallas_call(functools.partial(next_kernel, k) if k else first_kernel,...]
    pallas_call x1, Pallas kernels: 23.2 us -> 22.1 us  [local(): pl.pallas_call(second_kernel, out_shape=[stack, jax.ShapeDtypeStruct((cyc...]
  transfers between devices with their start and end apart: 4 -> 4, of which waited for: 1 -> 1; matrix products, arithmetic and copies ran while one was open for 0% -> 0% of each run, Pallas kernels for 33% -> 32%
where the time goes in v7:
time: 51 us; the launch traced here: 50.1 us
  Pallas kernels  39.2 us (77%)
  starting transfers between devices  7.19 us (14%)
  waiting for transfers between devices  2.38 us (5%)
  between operations  1.03 us (2%)
    pallas_call x1, Pallas kernels, local(): pl.pallas_call(second_kernel, out_shape=[stack, jax.ShapeDtypeStruct((cyc...  22.1 us
    pallas_call x4, Pallas kernels, local(): pl.pallas_call(functools.partial(next_kernel, k) if k else first_kernel,...  16.1 us
    ppermute x3, starting transfers between devices, local(): late = lax.ppermute(got, 'row', pairs[k]) if k < len(pairs) - 1 else None  7.12 us
    ppermute x3, waiting for transfers between devices, local(): late = lax.ppermute(got, 'row', pairs[k]) if k < len(pairs) - 1 else None  2.38 us
    pallas_call x1, Pallas kernels, local(): pl.pallas_call(pack_kernel, out_shape=jax.ShapeDtypeStruct((packed_size,...  1.09 us
  transfers between devices with their start and end apart: 4, of which 1 were waited for; matrix products, arithmetic and copies ran while one was open for 0% of the time, Pallas kernels for 32%

profile of v7, /device:TPU:0, one launch (start us, length us, event | category | flops | bytes accessed | tf_op | source)
XLA Modules:
  0.0 50.1 jit_solution(16691556590470854313)
XLA Ops:
  0.6 1.1 %pack.1 = bf16[1040,128]{1,0:T(8,128)(2,1)S(1)} custom-call(s32[2,8]{1,0:T(2,128)} %bitcast.6, s32[8,1,512]{2,1,0:T(1,128)} %label_rows.1, bf16[8,1,512,128]{3,2,1,0:T(8,128)(2,1)} %u0.1, bf16[8,1,512,128]{3,2,1,0:T(8,128)(2,1)} %v0.1), custom_call_target="tpu_custom_call" | custom-call | tf_op jit(solution)/shard_map/pack/pallas_call | solution.py:412
  1.7 3.9 %collective-permute-start = (bf16[1040,128]{1,0:T(8,128)(2,1)S(1)}, bf16[1040,128]{1,0:T(8,128)(2,1)S(1)}, u32[]{:S(2)}, u32[]{:S(2)}) collective-permute-start(bf16[1040,128]{1,0:T(8,128)(2,1)S(1)} %pack.1), channel_id=1, source_target_pairs={{1,9},{0,2},{17,25},{16,18}} | collective-permute-start | bytes 798728 | tf_op jit(solution)/shard_map/ppermute | solution.py:429
  5.6 4.9 %first0.1 = (f32[512,512]{1,0:T(8,128)S(1)}, f32[2,512,512]{2,1,0:T(8,128)}) custom-call(s32[3,2,512]{2,1,0:T(2,128)} %bitcast.4), custom_call_target="tpu_custom_call" | custom-call | flops 4000000000 | bytes 1000000 | tf_op jit(solution)/shard_map/first0/pallas_call | solution.py:430
  10.5 0.0 collective-permute-done
  10.5 0.1 add.9
  10.6 1.8 %collective-permute-start.1 = (bf16[1040,128]{1,0:T(8,128)(2,1)S(1)}, bf16[1040,128]{1,0:T(8,128)(2,1)S(1)}, u32[]{:S(2)}, u32[]{:S(2)}) collective-permute-start(bf16[1040,128]{1,0:T(8,128)(2,1)S(1)} %add.9), channel_id=1, source_target_pairs={{1,5},{9,13},{0,8},{2,10},{17,21},{25,29},{16,24},{18,26}} | collective-permute-start | bytes 798728 | tf_op jit(solution)/shard_map/ppermute | solution.py:429
  12.4 3.9 %first1.1 = (f32[512,512]{1,0:T(8,128)S(1)}, f32[2,512,512]{2,1,0:T(8,128)}) custom-call(f32[512,512]{1,0:T(8,128)S(1)} %get-tuple-element.20.old, f32[2,512,512]{2,1,0:T(8,128)} %get-tuple-element.21._), custom_call_target="tpu_custom_call", output_to_operand_aliasing={{0}: (0, {}), {1}: (1, {})} | custom-call | flops 4000000000 | bytes 1000000 | tf_op jit(solution)/shard_map/first1/pallas_call | solution.py:430
  16.3 2.4 %collective-permute-done.1 = bf16[1040,128]{1,0:T(8,128)(2,1)S(1)} collective-permute-done((bf16[1040,128]{1,0:T(8,128)(2,1)S(1)}, bf16[1040,128]{1,0:T(8,128)(2,1)S(1)}, u32[]{:S(2)}, u32[]{:S(2)}) %collective-permute-start.1) | collective-permute-done | bytes 266272 | tf_op jit(solution)/shard_map/ppermute | solution.py:429
  18.6 0.1 add.10
  18.7 1.5 %collective-permute-start.2 = (bf16[1040,128]{1,0:T(8,128)(2,1)S(1)}, bf16[1040,128]{1,0:T(8,128)(2,1)S(1)}, u32[]{:S(2)}, u32[]{:S(2)}) collective-permute-start(bf16[1040,128]{1,0:T(8,128)(2,1)S(1)} %add.10), channel_id=1, source_target_pairs={{1,3},{9,11},{5,7},{13,15},{0,4},{2,6},{8,12},{10,14},{17,19},{25,... | collective-permute-start | bytes 798728 | tf_op jit(solution)/shard_map/ppermute | solution.py:429
  20.2 3.8 %first2.1 = (f32[512,512]{1,0:T(8,128)S(1)}, f32[2,512,512]{2,1,0:T(8,128)}) custom-call(f32[512,512]{1,0:T(8,128)S(1)} %get-tuple-element.24.old, f32[2,512,512]{2,1,0:T(8,128)} %get-tuple-element.25._), custom_call_target="tpu_custom_call", output_to_operand_aliasing={{0}: (0, {}), {1}: (1, {})} | custom-call | flops 4000000000 | bytes 1000000 | tf_op jit(solution)/shard_map/first2/pallas_call | solution.py:430
  24.0 0.0 collective-permute-done.2
  24.0 0.1 add.11.got
  24.1 0.1 collective-permute-start.3
  24.1 0.0 copy-start
  24.2 0.0 copy-start.1
  24.2 0.0 copy-start.2
  24.2 0.0 copy-start.3
  24.2 0.0 copy-start.4
  24.2 0.0 copy-start.5
  24.2 0.0 copy-start.6
  24.2 3.5 %first3.1 = (f32[512,512]{1,0:T(8,128)S(1)}, f32[2,512,512]{2,1,0:T(8,128)}) custom-call(f32[512,512]{1,0:T(8,128)S(1)} %get-tuple-element.28.old, f32[2,512,512]{2,1,0:T(8,128)} %get-tuple-element.29._), custom_call_target="tpu_custom_call", output_to_operand_aliasing={{0}: (0, {}), {1}: (1, {})} | custom-call | flops 4000000000 | bytes 1000000 | tf_op jit(solution)/shard_map/first3/pallas_call | solution.py:430
  27.8 0.0 collective-permute-done.3.came
  27.8 0.0 copy-done
  27.8 0.0 copy-done.1
  27.8 0.0 copy-done.2
  27.8 0.0 copy-done.3
  27.8 0.0 copy-done.4
  27.8 0.0 copy-done.5
  27.8 0.0 copy-done.6
  27.9 22.1 %second.1 = (f32[2,512,512]{2,1,0:T(8,128)}, f32[8,1,512,256]{3,2,1,0:T(8,128)}) custom-call(s32[3,2,512]{2,1,0:T(2,128)S(1)} %bitcast.5, s32[2,8]{1,0:T(2,128)S(1)} %bitcast.7, s32[8,1,512]{2,1,0:T(1,128)S(1)} %copy-done.4, bf16[1040,128]{1,0:T(8,128)(2,1)S(1)} %add.11.got, ...), custom_call_target="tpu_custom_call", output_to_operand_aliasing={{0}: (10, {})} | custom-call | tf_op jit(solution)/shard_map/second/pallas_call | solution.py:451
Async XLA Ops:
  1.7 8.8 %collective-permute-start = (bf16[1040,128]{1,0:T(8,128)(2,1)S(1)}, bf16[1040,128]{1,0:T(8,128)(2,1)S(1)}, u32[]{:S(2)}, u32[]{:S(2)}) collective-permute-start(bf16[1040,128]{1,0:T(8,128)(2,1)S(1)} %pack.1), channel_id=1, source_target_pairs={{1,9},{0,2},{17,25},{16,18}} | collective-permute-start | bytes 798728 | tf_op jit(solution)/shard_map/ppermute | solution.py:429
  10.6 8.0 %collective-permute-start.1 = (bf16[1040,128]{1,0:T(8,128)(2,1)S(1)}, bf16[1040,128]{1,0:T(8,128)(2,1)S(1)}, u32[]{:S(2)}, u32[]{:S(2)}) collective-permute-start(bf16[1040,128]{1,0:T(8,128)(2,1)S(1)} %add.9), channel_id=1, source_target_pairs={{1,5},{9,13},{0,8},{2,10},{17,21},{25,29},{16,24},{18,26}} | collective-permute-start | bytes 798728 | tf_op jit(solution)/shard_map/ppermute | solution.py:429
  18.7 5.3 %collective-permute-start.2 = (bf16[1040,128]{1,0:T(8,128)(2,1)S(1)}, bf16[1040,128]{1,0:T(8,128)(2,1)S(1)}, u32[]{:S(2)}, u32[]{:S(2)}) collective-permute-start(bf16[1040,128]{1,0:T(8,128)(2,1)S(1)} %add.10), channel_id=1, source_target_pairs={{1,3},{9,11},{5,7},{13,15},{0,4},{2,6},{8,12},{10,14},{17,19},{25,... | collective-permute-start | bytes 798728 | tf_op jit(solution)/shard_map/ppermute | solution.py:429
  24.1 3.7 %collective-permute-start.3 = (bf16[1040,128]{1,0:T(8,128)(2,1)S(1)}, bf16[1040,128]{1,0:T(8,128)(2,1)S(1)}, u32[]{:S(2)}, u32[]{:S(2)}) collective-permute-start(bf16[1040,128]{1,0:T(8,128)(2,1)S(1)} %add.11.got), channel_id=1, source_target_pairs={{0,1},{1,0},{2,3},{3,2},{4,5},{5,4},{6,7},{7,6},{8,9},{9,8},{10,11... | collective-permute-start | bytes 798728 | tf_op jit(solution)/shard_map/ppermute | solution.py:449
  24.1 3.6 %copy-start = (bf16[8,1,512,128]{3,2,1,0:T(8,128)(2,1)S(1)}, bf16[8,1,512,128]{3,2,1,0:T(8,128)(2,1)}, u32[]{:S(2)}) copy-start(bf16[8,1,512,128]{3,2,1,0:T(8,128)(2,1)} %u0.1) | copy-start | bytes 3145732
  24.2 3.6 %copy-start.1 = (bf16[8,1,512,128]{3,2,1,0:T(8,128)(2,1)S(1)}, bf16[8,1,512,128]{3,2,1,0:T(8,128)(2,1)}, u32[]{:S(2)}) copy-start(bf16[8,1,512,128]{3,2,1,0:T(8,128)(2,1)} %v0.1) | copy-start | bytes 3145732
  24.2 3.6 %copy-start.2 = (bf16[8,1,512,128]{3,2,1,0:T(8,128)(2,1)S(1)}, bf16[8,1,512,128]{3,2,1,0:T(8,128)(2,1)}, u32[]{:S(2)}) copy-start(bf16[8,1,512,128]{3,2,1,0:T(8,128)(2,1)} %u1_.1) | copy-start | bytes 3145732
  24.2 3.6 %copy-start.3 = (bf16[8,1,512,128]{3,2,1,0:T(8,128)(2,1)S(1)}, bf16[8,1,512,128]{3,2,1,0:T(8,128)(2,1)}, u32[]{:S(2)}) copy-start(bf16[8,1,512,128]{3,2,1,0:T(8,128)(2,1)} %v1.1) | copy-start | bytes 3145732
  24.2 3.6 %copy-start.4 = (s32[8,1,512]{2,1,0:T(1,128)S(1)}, s32[8,1,512]{2,1,0:T(1,128)}, u32[]{:S(2)}) copy-start(s32[8,1,512]{2,1,0:T(1,128)} %label_rows.1) | copy-start | bytes 49156
  24.2 3.6 %copy-start.5 = (s32[2,3,512]{2,0,1:T(2,128)S(1)}, s32[2,3,512]{2,0,1:T(2,128)}, u32[]{:S(2)}) copy-start(s32[2,3,512]{2,0,1:T(2,128)} %param.7) | copy-start | bytes 36868
  24.2 3.6 %copy-start.6 = (s32[8,1,2]{0,2,1:T(2,128)S(1)}, s32[8,1,2]{0,2,1:T(2,128)}, u32[]{:S(2)}) copy-start(s32[8,1,2]{0,2,1:T(2,128)} %param.9) | copy-start | bytes 196
